TPU v7x, 128 devices: a whole 4x4x4 slice. The times are simulated.
128 devices in a mesh: dp: 16 (over x, z), seq: 8 (over y, core).
Axes of the slice: x: 4, y: 4, z: 4, core: 2. Of those that a mesh axis runs over, the one named last changes fastest.
Arguments:
- waveforms: float32 [256, 40960], P(('dp', 'seq')), may hold values from -6 to 6
- utt_len: int32 [64, 4], P('dp'), may hold values from 5120 to 40960, as said below
- pack_order: int32 [64, 4], P('dp'), may hold values from 0 to 3, each once within a row
- conv_first: float32 [10, 512], replicated, may hold values from -2 to 2
- conv_mid: bfloat16 [4, 3, 512, 512], replicated, may hold values from -0.15625 to 0.15625
- conv_last: bfloat16 [2, 2, 512, 512], replicated, may hold values from -0.1875 to 0.1875
- conv_bias: float32 [7, 512], replicated, may hold values from -3 to 3
- conv_gain: float32 [7, 512], replicated, may hold values from 0.1 to 1.9
- conv_shift: float32 [7, 512], replicated, may hold values from -3 to 3
- proj_gain: float32 [512], replicated, may hold values from 0.1 to 1.9
- proj_shift: float32 [512], replicated, may hold values from -3 to 3
- proj_weight: bfloat16 [512, 1024], replicated, may hold values from -0.25 to 0.25
- proj_bias: float32 [1024], replicated, may hold values from -3 to 3
- conf_gain: float32 [2, 1024], replicated, may hold values from 0.1 to 1.9
- conf_up: bfloat16 [2, 1024, 2048], replicated, may hold values from -0.1875 to 0.1875
- conf_depth: float32 [2, 31, 1024], replicated, may hold values from -1 to 1
- depth_bias: float32 [2, 1024], replicated, may hold values from -3 to 3
- conf_down: bfloat16 [2, 1024, 1024], replicated, may hold values from -0.1875 to 0.1875
Outputs:
- encoded: bfloat16 [64, 512, 1024], P('dp', 'seq')
Inputs may be any that keep to these rules, and one draw needn't show every extreme that they name: `utt_len`: valid samples of each slot; in every draw some slot has exactly 40960. `pack_order`: each row lists 0 to 3 once.
All inputs are finite; a program needn't handle non-finite values.
Results may differ from a plain program's by a relative error of at most 0.02.
Values may be sent and summed in bfloat16 or wider, within the bound.
A program may use at most 128 MiB of HBM per device.

v0:
```python
import jax
import jax.numpy as jnp
from jax import lax
from jax.experimental import pallas as pl
from jax.experimental.pallas import tpu as pltpu
from jax.sharding import PartitionSpec as P

EPS = 1e-05
SEG_MAX = 8
NPH = 18
QC = (0.79787296, 0.036364917, -5.735435e-05, -4.7398415e-05, 2.8125112e-06, -5.711017e-08)
QH = tuple(2.0 * c * 4.0 ** i for i, c in enumerate(QC))


def half_gelu(h):
    u = jnp.minimum(h * h, 6.25)
    q = QH[5]
    for c in QH[4::-1]:
        q = q * u + c
    return h + h * jnp.tanh(h * q)


def finish(v, gain, shift):
    ss = jnp.sum(v * v, axis=-1, keepdims=True)
    r = lax.rsqrt(ss * (1.0 / 512) + EPS)
    return half_gelu((v * r) * gain + shift).astype(jnp.bfloat16)


def encoder_kernel(lens, order, utts, taps, wmid, wlast, bias, gain, shift, pgain, pshift, out,
                   packed, lhs, y0, y1, e1, e2, e3, e4, e5, e6, out32):
    f32 = jnp.float32
    seq = lax.axis_index("seq")
    own, core = seq // 2, seq % 2
    packed[...] = jnp.zeros_like(packed)
    lane = lax.broadcasted_iota(jnp.int32, (320, 128), 1)
    sample = lax.broadcasted_iota(jnp.int32, (320, 128), 0) * 128 + lane
    off = jnp.int32(0)
    for p in range(4):
        u = order[own, p]
        ln = lens[own, u]
        a, b = off // 128, off % 128
        seg = jnp.where(sample < ln, utts[u].astype(f32), 0.0)
        rolled = pltpu.roll(seg, b, 1)
        packed[pl.ds(a, 320), :] += jnp.where(lane >= b, rolled, 0.0)
        packed[pl.ds(a + 1, 320), :] += jnp.where(lane < b, rolled, 0.0)
        off = off + ln
    nv = ((off + 10239) // 10240 - core + 1) // 2

    def row(ref, l):
        return ref[pl.ds(l, 1), :]

    def dot_(a, b):
        return jnp.dot(a, b, preferred_element_type=f32)

    def epi(y, l, groups, dst, with_bias=True):
        g, s = row(gain, l), row(shift, l)
        b = row(bias, l) if with_bias else None
        for k in range(groups):
            v = y[pl.ds(16 * k, 16), :]
            if with_bias:
                v = v + b
            dst(k, finish(v, g, s))

    def conv3(src, l, start, rows, gap, y):
        y[pl.ds(0, rows), :] = dot_(src[pl.ds(start, rows), :], wmid[l, 0:1024, :]) + dot_(
            src[pl.ds(start + gap, rows), 0:512], wmid[l, 1024:1536, :])

    def put(ref, gap, base=0):
        def at(k, v):
            ref[pl.ds((k // 2) * gap + base, 16), (k % 2) * 512:(k % 2) * 512 + 512] = v
        return at

    def chain(l, x):
        return dot_(x, wmid[l, 0:512, :]) + dot_(x, wmid[l, 512:1024, :]) + dot_(x, wmid[l, 1024:1536, :])
    x = finish(jnp.broadcast_to(row(bias, 0), (16, 512)), row(gain, 0), row(shift, 0))
    for l in range(3):
        x = finish(chain(l, x) + row(bias, l + 1), row(gain, l + 1), row(shift, l + 1))

    def fill(i, _):
        for k in range(NPH):
            e4[pl.ds((k // 2) * 128 + 16 * i, 16), (k % 2) * 512:(k % 2) * 512 + 512] = x
        return 0
    lax.fori_loop(nv, SEG_MAX, fill, 0)

    lane16 = lax.broadcasted_iota(jnp.int32, (16, 128), 1)

    def segment(i, _):
        base = 5 * (32 * i + 16 * core)
        cols = [packed[pl.ds(base + j, 16, stride=5), :] for j in range(6)]
        for q in range(NPH):
            j, o = divmod(40 * q, 128)
            w = cols[j] if o == 0 else pltpu.roll(cols[j], 128 - o, 1)
            if o + 45 > 128:
                w = jnp.where(lane16 < 128 - o, w, pltpu.roll(cols[j + 1], 128 - o, 1))
            w = jnp.where(lane16 >= 126, 1.0, w)
            lhs[pl.ds(16 * q, 16), :] = w.astype(jnp.bfloat16)

        def first(v, y):
            y[...] = dot_(lhs[...], taps[v])

        def put1(j, half):
            def at(q, val):
                e1[pl.ds(pl.multiple_of(64 * q + 16 * j, 16), 16), 512 * half:512 * half + 512] = val
            return at
        first(0, y0)

        def pair(j, _):
            first(2 * j + 1, y1)
            epi(y0, 0, NPH, put1(j, 0), False)
            first(jnp.minimum(2 * j + 2, 7), y0)
            epi(y1, 0, NPH, put1(j, 1), False)
            return 0
        lax.fori_loop(0, 4, pair, 0)

        n = 16 * NPH
        conv3(e1, 0, 0, n, 16, y0)
        conv3(e1, 0, n, n, 16, y1)
        epi(y0, 1, NPH, put(e2, 16, 0))
        conv3(e1, 0, 2 * n, n, 16, y0)
        epi(y1, 1, NPH, put(e2, 16, n // 2))
        conv3(e1, 0, 3 * n, n, 16, y1)
        epi(y0, 1, NPH, put(e2, 16, n))
        conv3(e2, 1, 0, n, 16, y0)
        epi(y1, 1, NPH, put(e2, 16, 3 * n // 2))
        conv3(e2, 1, n, n, 16, y1)
        epi(y0, 2, NPH, put(e3, 16, 0))
        epi(y1, 2, NPH, put(e3, 16, n // 2))
        conv3(e3, 2, 0, n, 16, y0)
        epi(y0, 3, NPH, put(e4, 128, pl.multiple_of(16 * i, 16)))
        return 0
    lax.fori_loop(0, nv, segment, 0)

    def conv2(src, l, start, y):
        y[pl.ds(0, 256), :] = dot_(src[pl.ds(start, 256), :], wlast[l])

    def put8(ref, base):
        def at(k, v):
            ref[pl.ds(base + 16 * (k % 8), 16), (k // 8) * 512:(k // 8) * 512 + 512] = v
        return at
    conv3(e4, 3, 0, 256, 128, y0)
    conv3(e4, 3, 256, 256, 128, y1)
    epi(y0, 4, 16, put8(e5, 0))
    conv3(e4, 3, 512, 256, 128, y0)
    epi(y1, 4, 16, put8(e5, 128))
    conv3(e4, 3, 768, 256, 128, y1)
    epi(y0, 4, 16, put8(e5, 256))
    conv2(e5, 0, 0, y0)
    epi(y1, 4, 16, put8(e5, 384))
    conv2(e5, 0, 256, y1)
    epi(y0, 5, 16, put8(e6, 0))
    epi(y1, 5, 16, put8(e6, 128))
    conv2(e6, 1, 0, y0)

    pg, ps = pgain[...], pshift[...]

    def last(k, v):
        v = v.astype(f32)
        v = v - jnp.mean(v, axis=-1, keepdims=True)
        v = v * lax.rsqrt(jnp.mean(v * v, axis=-1, keepdims=True) + EPS) * pg + ps
        for c in range(4):
            out32[c, pl.ds(32 * (k % 8) + k // 8, 16, stride=2), :] = v[:, 128 * c:128 * c + 128]
    epi(y0, 6, 16, last)
    out[0:32, :] = jnp.zeros((32, 512), jnp.bfloat16)
    out[288:320, :] = jnp.zeros((32, 512), jnp.bfloat16)
    for c in range(4):
        out[32:288, 128 * c:128 * c + 128] = out32[c].astype(jnp.bfloat16)


def prepare(conv_first, conv_mid, conv_last, conv_bias):
    bf16, f32 = jnp.bfloat16, jnp.float32
    def centre(w):
        w = w.astype(f32)
        return w - jnp.mean(w, axis=-1, keepdims=True)
    bias = centre(conv_bias)
    first = centre(conv_first).astype(bf16)
    hi = bias[0].astype(bf16)
    lo = (bias[0] - hi.astype(f32)).astype(bf16)
    tail = jnp.stack([hi, lo])
    taps = jnp.stack([
        jnp.concatenate([jnp.zeros((5 * v, 512), bf16), first, jnp.zeros((116 - 5 * v, 512), bf16), tail])
        for v in range(8)])
    wmid = centre(conv_mid).astype(bf16).reshape(4, 1536, 512)
    wlast = centre(conv_last).astype(bf16).reshape(2, 1024, 512)
    return taps, wmid, wlast, bias


def encode(lens, order, utts, taps, wmid, wlast, bias, gain, shift, pgain, pshift):
    bf16, f32 = jnp.bfloat16, jnp.float32
    vm = pl.BlockSpec(memory_space=pltpu.VMEM)
    sm = pl.BlockSpec(memory_space=pltpu.SMEM)
    return pl.pallas_call(
        encoder_kernel,
        out_shape=jax.ShapeDtypeStruct((320, 512), bf16),
        in_specs=[sm, sm] + [vm] * 9,
        out_specs=vm,
        scratch_shapes=[
            pltpu.VMEM((1296, 128), f32),
            pltpu.VMEM((288, 128), bf16),
            pltpu.VMEM((288, 512), f32),
            pltpu.VMEM((288, 512), f32),
            pltpu.VMEM((73 * 16, 1024), bf16),
            pltpu.VMEM((37 * 16, 1024), bf16),
            pltpu.VMEM((19 * 16, 1024), bf16),
            pltpu.VMEM((9 * 128, 1024), bf16),
            pltpu.VMEM((4 * 128, 1024), bf16),
            pltpu.VMEM((2 * 128, 1024), bf16),
            pltpu.VMEM((4, 256, 128), f32),
        ],
        compiler_params=pltpu.CompilerParams(vmem_limit_bytes=40 << 20),
        name="encode",
    )(lens, order, utts, taps, wmid, wlast, bias, gain * 0.5, shift * 0.5, pgain, pshift)


MESH = pl.DeviceIdType.MESH


def audio_kernel(waves, out, stage, held, ssem, rsem):
    dp, seq = lax.axis_index("dp"), lax.axis_index("seq")
    mine = seq == dp // 2
    barrier = pltpu.get_barrier_semaphore()

    def source(k):
        return {"dp": 4 * (seq // 2) + k, "seq": dp // 2}

    for k in range(4):
        @pl.when(jnp.logical_not(jnp.logical_and(mine, dp % 4 == k)))
        def _():
            pl.semaphore_signal(barrier, inc=1, device_id=source(k), device_id_type=MESH)

    def unfold(i, _):
        for e in range(2):
            stage[e, pl.ds(i, 1), :] = waves[e:e + 1, pl.ds(pl.multiple_of(128 * i, 128), 128)]
        return 0
    lax.fori_loop(0, 320, unfold, 0)
    held[...] = stage[...].astype(jnp.bfloat16)
    pl.semaphore_wait(barrier, jnp.where(mine, 3, 4))
    slot = dp % 4

    def copy(e, c):
        return pltpu.make_async_remote_copy(
            src_ref=held.at[e], dst_ref=out.at[slot],
            send_sem=ssem.at[2 * e + c], recv_sem=rsem.at[slot],
            device_id={"dp": 2 * seq + e, "seq": 2 * (dp // 4) + c}, device_id_type=MESH)

    def here(e, c):
        return jnp.logical_and(mine, jnp.logical_and(dp % 2 == e, seq % 2 == c))

    for e in range(2):
        for c in range(2):
            @pl.when(jnp.logical_not(here(e, c)))
            def _():
                copy(e, c).start()

            @pl.when(here(e, c))
            def _():
                out[slot] = held[e]
    for k in range(4):
        @pl.when(jnp.logical_not(jnp.logical_and(mine, slot == k)))
        def _():
            pltpu.make_async_remote_copy(
                src_ref=held.at[0], dst_ref=out.at[k], send_sem=ssem.at[0], recv_sem=rsem.at[k],
                device_id=source(k), device_id_type=MESH).wait_recv()
    for e in range(2):
        for c in range(2):
            @pl.when(jnp.logical_not(here(e, c)))
            def _():
                copy(e, c).wait_send()


def exchange_audio(waves):
    vm = pl.BlockSpec(memory_space=pltpu.VMEM)
    return pl.pallas_call(
        audio_kernel,
        out_shape=jax.ShapeDtypeStruct((4, 320, 128), jnp.bfloat16),
        in_specs=[vm],
        out_specs=vm,
        scratch_shapes=[
            pltpu.VMEM((2, 320, 128), jnp.float32),
            pltpu.VMEM((2, 320, 128), jnp.bfloat16),
            pltpu.SemaphoreType.DMA((4,)),
            pltpu.SemaphoreType.DMA((4,)),
        ],
        compiler_params=pltpu.CompilerParams(collective_id=1, has_side_effects=True),
        name="audio",
    )(waves)


def frames_kernel(frames, out, ssem, rsem):
    seq = lax.axis_index("seq")
    barrier = pltpu.get_barrier_semaphore()
    for o in range(1, 8):
        pl.semaphore_signal(barrier, inc=1, device_id={"seq": (seq + o) % 8}, device_id_type=MESH)

    def piece(d):
        return pl.ds(pl.multiple_of(32 * d + 32 * (1 - seq % 2), 32), 64)

    def copy(o):
        d = (seq + o) % 8
        return pltpu.make_async_remote_copy(
            src_ref=frames.at[piece(d)], dst_ref=out.at[seq],
            send_sem=ssem.at[o], recv_sem=rsem.at[seq],
            device_id={"seq": d}, device_id_type=MESH)
    pl.semaphore_wait(barrier, 7)
    for o in range(1, 8):
        copy(o).start()
    out[seq] = frames[piece(seq), :]
    for o in range(1, 8):
        d = (seq + o) % 8
        pltpu.make_async_remote_copy(
            src_ref=frames.at[piece(d)], dst_ref=out.at[d], send_sem=ssem.at[o], recv_sem=rsem.at[d],
            device_id={"seq": d}, device_id_type=MESH).wait_recv()
    for o in range(1, 8):
        copy(o).wait_send()


def exchange_frames(frames):
    vm = pl.BlockSpec(memory_space=pltpu.VMEM)
    return pl.pallas_call(
        frames_kernel,
        out_shape=jax.ShapeDtypeStruct((8, 64, 512), jnp.bfloat16),
        in_specs=[vm],
        out_specs=vm,
        scratch_shapes=[pltpu.SemaphoreType.DMA((8,)), pltpu.SemaphoreType.DMA((8,))],
        compiler_params=pltpu.CompilerParams(collective_id=2, has_side_effects=True),
        name="frames",
    )(frames)


def conformer_kernel(lens, recv, wp, pb, gain, up, taps, dbias, down, out,
                     nrm, s0, s1, lifted, ya, yb, g, act):
    f32, bf16 = jnp.float32, jnp.bfloat16
    base = 64 * lax.axis_index("seq") - 32
    for r in range(4):
        for c in range(4):
            nrm[128 * r + 32 * c:128 * r + 32 * c + 32, :] = recv[2 * r + (c + 1) % 2, 32 * (c // 2):32 * (c // 2) + 32, :]

    def dot_(a, b):
        return jnp.dot(a, b, preferred_element_type=f32)

    for n in range(4):
        w = slice(256 * n, 256 * n + 256)
        s0[:, w] = dot_(nrm[...], wp[:, w]) + pb[:, w]

    def norm(src, l, rows):
        gl = gain[l:l + 1, :]

        def body(i, _):
            at = pl.ds(pl.multiple_of(16 * i, 16), 16)
            v = src[at, :]
            v = v - jnp.mean(v, axis=-1, keepdims=True)
            v = v * lax.rsqrt(jnp.mean(v * v, axis=-1, keepdims=True) + EPS) * gl
            lifted[at, :] = v.astype(bf16)
            return 0
        lax.fori_loop(0, rows // 16, body, 0, unroll=2)

    def module(l, per, lo, keep):
        rows = 4 * per

        def chunk(n, _):
            wa = pl.ds(pl.multiple_of(256 * n, 256), 256)
            wb = pl.ds(pl.multiple_of(1024 + 256 * n, 256), 256)
            ya[0:rows, :] = dot_(lifted[0:rows, :], up[l, :, wa])
            yb[0:rows, :] = dot_(lifted[0:rows, :], up[l, :, wb])
            for r in range(4):
                total = lens[r, 0] + lens[r, 1] + lens[r, 2] + lens[r, 3]
                valid = (total - 400) // 320 + 1
                for k in range(per // 16):
                    at = slice(per * r + 16 * k, per * r + 16 * k + 16)
                    t = base + lo + 16 * k + lax.broadcasted_iota(jnp.int32, (16, 256), 0)
                    live = jnp.logical_and(t >= 0, t < valid)
                    v = jnp.where(live, ya[at, :] * jax.nn.sigmoid(yb[at, :]), 0.0)
                    g[2 * n, r, lo + 16 * k:lo + 16 * k + 16, :] = v[:, 0:128]
                    g[2 * n + 1, r, lo + 16 * k:lo + 16 * k + 16, :] = v[:, 128:256]
            return 0
        lax.fori_loop(0, 4, chunk, 0)
        first = 64 - keep // 2

        def depth(c, _):
            w = pl.ds(pl.multiple_of(128 * c, 128), 128)

            def one(r, _):
                acc = jnp.broadcast_to(dbias[l:l + 1, w], (keep, 128))
                for j in range(31):
                    acc = acc + g[c, r, first + j - 15:first + j - 15 + keep, :] * taps[l, j:j + 1, w]
                act[pl.ds(pl.multiple_of(keep * r, 32), keep), w] = (acc * jax.nn.sigmoid(acc)).astype(bf16)
                return 0
            return lax.fori_loop(0, 4, one, 0)
        lax.fori_loop(0, 8, depth, 0)

    norm(s0, 0, 512)
    module(0, 128, 0, 96)
    for n in range(4):
        w = slice(256 * n, 256 * n + 256)
        d = dot_(act[...], down[0, :, w])
        for r in range(4):
            s1[96 * r:96 * r + 96, w] = s0[128 * r + 16:128 * r + 112, w] + d[96 * r:96 * r + 96]
    norm(s1, 1, 384)
    module(1, 96, 16, 64)
    for n in range(4):
        w = slice(256 * n, 256 * n + 256)
        d = dot_(act[0:256, :], down[1, :, w])
        for r in range(4):
            out[r, :, w] = (s1[96 * r + 16:96 * r + 80, w] + d[64 * r:64 * r + 64]).astype(bf16)


def conform(lens, recv, wp, pb, gain, up, taps, dbias, down):
    bf16, f32 = jnp.bfloat16, jnp.float32
    vm = pl.BlockSpec(memory_space=pltpu.VMEM)
    return pl.pallas_call(
        conformer_kernel,
        out_shape=jax.ShapeDtypeStruct((4, 64, 1024), bf16),
        in_specs=[pl.BlockSpec(memory_space=pltpu.SMEM)] + [vm] * 8,
        out_specs=vm,
        scratch_shapes=[
            pltpu.VMEM((512, 512), bf16),
            pltpu.VMEM((512, 1024), f32),
            pltpu.VMEM((384, 1024), f32),
            pltpu.VMEM((512, 1024), bf16),
            pltpu.VMEM((512, 256), f32),
            pltpu.VMEM((512, 256), f32),
            pltpu.VMEM((8, 4, 128, 128), f32),
            pltpu.VMEM((384, 1024), bf16),
        ],
        compiler_params=pltpu.CompilerParams(vmem_limit_bytes=40 << 20),
        name="conform",
    )(lens, recv, wp, pb, gain, up, taps, dbias, down)


def per_device(waveforms, utt_len, pack_order, conv_first, conv_mid, conv_last, conv_bias, conv_gain,
               conv_shift, proj_gain, proj_shift, proj_weight, proj_bias, conf_gain, conf_up,
               conf_depth, depth_bias, conf_down):
    utts = exchange_audio(waveforms)
    frames = encode(utt_len, pack_order, utts, *prepare(conv_first, conv_mid, conv_last, conv_bias),
                    conv_gain, conv_shift, proj_gain[None], proj_shift[None])
    recv = exchange_frames(frames)
    return conform(utt_len, recv, proj_weight, proj_bias[None], conf_gain, conf_up, conf_depth,
                   depth_bias, conf_down)


def solution(mesh):
    return jax.shard_map(
        per_device,
        mesh=mesh,
        in_specs=(P(("dp", "seq"), None), P("dp", None), P("dp", None)) + (P(),) * 15,
        out_specs=P("dp", "seq", None),
        check_vma=False,
    )
```

profile of v0, /device:TPU:71, one launch (start us, length us, event | category | flops | bytes accessed | tf_op | source)
XLA Modules:
  0.0 146.1 jit_solution(14877480971353740142)
XLA Ops:
  0.0 0.8 reduce_sum.37
  0.8 0.8 broadcast_subtract_fusion.bias
  1.6 0.9 reduce_sum.36
  2.5 0.8 subtract_convert_fusion
  3.4 0.1 pad.1.clone
  3.4 0.1 fusion.2
  3.6 0.5 concatenate.33
  4.1 0.4 concatenate.34
  4.6 0.4 concatenate.35
  5.0 0.4 concatenate.36
  5.5 0.4 concatenate.37
  6.0 0.2 concatenate.38
  6.2 0.4 concatenate.39
  6.7 0.9 broadcast_multiply_fusion.1
  7.6 3.9 %convert_reduce_fusion = f32[4,3,512]{2,1,0:T(4,128)S(1)} fusion(bf16[4,3,512,512]{3,2,1,0:T(8,128)(2,1)} %param.22), kind=kLoop, calls=%fused_computation.1 | loop fusion | flops 6285312 | bytes 6316032 | tf_op jit(solution)/shard_map/reduce_sum | solution.py:173
  11.4 0.0 copy-done.14
  11.5 0.0 copy-start.15
  11.5 3.6 %fusion = bf16[4,3,512,512]{3,2,1,0:T(8,128)(2,1)} fusion(bf16[4,3,512,512]{3,2,1,0:T(8,128)(2,1)S(1)} %copy-done.14, f32[4,3,512]{2,1,0:T(4,128)S(1)} %broadcast_multiply_fusion), kind=kLoop, calls=%fused_computation.2 | loop fusion | flops 9437184 | bytes 12607488 | tf_op jit(solution)/shard_map/convert_element_type | solution.py:182
  15.1 0.0 copy-done.15
  15.1 0.4 convert_reduce_fusion.1
  15.5 0.5 fusion.1
  16.0 0.0 copy-start.16
  16.0 0.0 copy-start.7
  16.0 0.0 copy-start.8
  16.0 0.0 copy-start.10
  16.0 21.2 %audio.1.utts = bf16[4,320,128]{2,1,0:T(8,128)(2,1)} custom-call(f32[2,40960]{1,0:T(2,128)} %waves.1), custom_call_target="tpu_custom_call" | custom-call | tf_op jit(solution)/shard_map/audio/pallas_call | solution.py:272
  37.2 0.0 copy-done.9
  37.2 0.0 copy-done.11
  37.3 0.0 copy-done.12
  37.3 0.0 copy-done.13
  37.3 0.0 copy-start
  37.3 2.8 %copy-done = bf16[4,3,512,512]{3,2,1,0:T(8,128)(2,1)S(1)} copy-done((bf16[4,3,512,512]{3,2,1,0:T(8,128)(2,1)S(1)}, bf16[4,3,512,512]{3,2,1,0:T(8,128)(2,1)}, u32[]{:S(2)}) %copy-start) | copy-done | bytes 6291480
  40.1 1.0 copy-done.5
  41.0 40.9 %encode.1.frames = bf16[320,512]{1,0:T(8,128)(2,1)S(1)} custom-call(s32[4,4]{1,0:T(4,128)S(1)} %copy-done.9, s32[4,4]{1,0:T(4,128)S(1)} %copy-done.11, bf16[4,320,128]{2,1,0:T(8,128)(2,1)S(1)} %copy-done.5, bf16[8,128,512]{2,1,0:T(8,128)(2,1)S(1)} %bitcast_dynamic-update-slice_fusion.taps, bf16[4,1536,512]{2,1,0:T(8,128)(2,1)S(1)} %bitcast.23, ...), custom_call_target="tpu_custom_call" | custom-call | tf_op jit(solution)/shard_map/encode/pallas_call | solution.py:191
  82.0 0.0 copy-start.4
  82.0 0.7 copy-done.4
  82.7 34.0 %frames.1.recv = bf16[8,64,512]{2,1,0:T(8,128)(2,1)} custom-call(bf16[320,512]{1,0:T(8,128)(2,1)} %copy-done.4), custom_call_target="tpu_custom_call" | custom-call | tf_op jit(solution)/shard_map/frames/pallas_call | solution.py:318
  116.7 0.0 copy-done.16
  116.7 0.1 copy.19.taps
  116.8 0.0 copy-done.7
  116.8 0.0 copy-done.8
  116.8 0.0 copy-done.10
  116.8 0.0 copy-start.1
  116.8 3.4 %copy-done.1 = bf16[2,1024,2048]{2,1,0:T(8,128)(2,1)S(1)} copy-done((bf16[2,1024,2048]{2,1,0:T(8,128)(2,1)S(1)}, bf16[2,1024,2048]{2,1,0:T(8,128)(2,1)}, u32[]{:S(2)}) %copy-start.1) | copy-done | bytes 8388632
  120.2 2.2 %copy-done.2 = bf16[2,1024,1024]{2,1,0:T(8,128)(2,1)S(1)} copy-done((bf16[2,1024,1024]{2,1,0:T(8,128)(2,1)S(1)}, bf16[2,1024,1024]{2,1,0:T(8,128)(2,1)}, u32[]{:S(2)}) %copy-start.2) | copy-done | bytes 4194328
  122.4 1.0 copy-done.3
  123.4 1.2 copy-done.6
  124.6 21.4 %conform.1 = bf16[4,64,1024]{2,1,0:T(8,128)(2,1)} custom-call(s32[4,4]{1,0:T(4,128)S(1)} %copy-done.9, bf16[8,64,512]{2,1,0:T(8,128)(2,1)S(1)} %copy-done.3, bf16[512,1024]{1,0:T(8,128)(2,1)S(1)} %copy-done.6, f32[1,1024]{1,0:T(1,128)S(1)} %bitcast.25, f32[2,1024]{1,0:T(2,128)S(1)} %copy-done.7, bf16[2,1024,2048]{2,1,0:T(8,128)(2,1)S(1)} %copy-done.1, ...), custom_call_target="tpu_custom_call" | custom-call | tf_op jit(solution)/shard_map/conform/pallas_call | solution.py:409
  (37 shorter events, 0.2 us)
Async XLA Ops:
  6.6 4.8 %copy-start.14 = (bf16[4,3,512,512]{3,2,1,0:T(8,128)(2,1)S(1)}, bf16[4,3,512,512]{3,2,1,0:T(8,128)(2,1)}, u32[]{:S(2)}) copy-start(bf16[4,3,512,512]{3,2,1,0:T(8,128)(2,1)} %param.22) | copy-start | bytes 18874372
  11.5 3.7 %copy-start.15 = (bf16[2,2,512,512]{3,2,1,0:T(8,128)(2,1)S(1)}, bf16[2,2,512,512]{3,2,1,0:T(8,128)(2,1)}, u32[]{:S(2)}) copy-start(bf16[2,2,512,512]{3,2,1,0:T(8,128)(2,1)} %param.23) | copy-start | bytes 6291460
  15.1 22.1 %copy-start.9 = (s32[4,4]{1,0:T(4,128)S(1)}, s32[4,4]{1,0:T(4,128)}, u32[]{:S(2)}) copy-start(s32[4,4]{1,0:T(4,128)} %lens.3) | copy-start | bytes 196
  15.1 22.1 %copy-start.11 = (s32[4,4]{1,0:T(4,128)S(1)}, s32[4,4]{1,0:T(4,128)}, u32[]{:S(2)}) copy-start(s32[4,4]{1,0:T(4,128)} %order.1) | copy-start | bytes 196
  15.1 22.2 %copy-start.12 = (f32[512]{0:T(512)S(1)}, f32[512]{0:T(512)}, u32[]{:S(2)}) copy-start(f32[512]{0:T(512)} %param.27) | copy-start | bytes 6148
  15.1 22.2 %copy-start.13 = (f32[512]{0:T(512)S(1)}, f32[512]{0:T(512)}, u32[]{:S(2)}) copy-start(f32[512]{0:T(512)} %param.28) | copy-start | bytes 6148
  16.0 100.7 %copy-start.16 = (f32[2,31,1024]{2,0,1:T(2,128)S(1)}, f32[2,31,1024]{2,0,1:T(2,128)}, u32[]{:S(2)}) copy-start(f32[2,31,1024]{2,0,1:T(2,128)} %param.33) | copy-start | bytes 761860
  16.0 100.8 %copy-start.7 = (f32[2,1024]{1,0:T(2,128)S(1)}, f32[2,1024]{1,0:T(2,128)}, u32[]{:S(2)}) copy-start(f32[2,1024]{1,0:T(2,128)} %gain.1) | copy-start | bytes 24580
  16.0 100.8 %copy-start.8 = (f32[2,1024]{1,0:T(2,128)S(1)}, f32[2,1024]{1,0:T(2,128)}, u32[]{:S(2)}) copy-start(f32[2,1024]{1,0:T(2,128)} %dbias.1) | copy-start | bytes 24580
  16.0 100.8 %copy-start.10 = (f32[1024]{0:T(1024)S(1)}, f32[1024]{0:T(1024)}, u32[]{:S(2)}) copy-start(f32[1024]{0:T(1024)} %param.30) | copy-start | bytes 12292
  37.3 2.8 %copy-start = (bf16[4,3,512,512]{3,2,1,0:T(8,128)(2,1)S(1)}, bf16[4,3,512,512]{3,2,1,0:T(8,128)(2,1)}, u32[]{:S(2)}) copy-start(bf16[4,3,512,512]{3,2,1,0:T(8,128)(2,1)} %fusion) | copy-start | bytes 18874372
  40.1 1.0 copy-start.5
  82.0 0.7 copy-start.4
  116.8 3.4 %copy-start.1 = (bf16[2,1024,2048]{2,1,0:T(8,128)(2,1)S(1)}, bf16[2,1024,2048]{2,1,0:T(8,128)(2,1)}, u32[]{:S(2)}) copy-start(bf16[2,1024,2048]{2,1,0:T(8,128)(2,1)} %up.1) | copy-start | bytes 25165828
  120.2 2.2 %copy-start.2 = (bf16[2,1024,1024]{2,1,0:T(8,128)(2,1)S(1)}, bf16[2,1024,1024]{2,1,0:T(8,128)(2,1)}, u32[]{:S(2)}) copy-start(bf16[2,1024,1024]{2,1,0:T(8,128)(2,1)} %down.1) | copy-start | bytes 12582916
  122.4 1.0 copy-start.3
  123.4 1.2 copy-start.6
where the time goes:
time: 147 us; the launch traced here: 146 us
  Pallas kernels  118 us (80%)
  local copies, waits for them, and re-layouts  15.5 us (11%)
  other arithmetic  12.7 us (9%)
    pallas_call x1, Pallas kernels, encode(): pl.pallas_call(encoder_kernel, out_shape=jax.ShapeDtypeStruct((320, 512),...  40.9 us
    pallas_call x1, Pallas kernels, exchange_frames(): pl.pallas_call(frames_kernel, out_shape=jax.ShapeDtypeStruct((8, 64, 512)...  34 us
    pallas_call x1, Pallas kernels, conform(): pl.pallas_call(conformer_kernel, out_shape=jax.ShapeDtypeStruct((4, 64, 1...  21.4 us
    pallas_call x1, Pallas kernels, exchange_audio(): pl.pallas_call(audio_kernel, out_shape=jax.ShapeDtypeStruct((4, 320, 128)...  21.2 us
    unnamed x41, local copies, waits for them, and re-layouts  12.5 us
    reduce_sum x4, other arithmetic, centre(): return w - jnp.mean(w, axis=-1, keepdims=True)  5.95 us
    convert_element_type x1, other arithmetic, prepare(): wmid = centre(conv_mid).astype(bf16).reshape(4, 1536, 512)  3.63 us

commit v1 on v0

v1 whole, which is shorter than its diff:
```python
import jax
import jax.numpy as jnp
from jax import lax
from jax.experimental import pallas as pl
from jax.experimental.pallas import tpu as pltpu
from jax.sharding import PartitionSpec as P

EPS = 1e-05
QH = tuple(2.0 * c * 4.0 ** i for i, c in enumerate((0.7976911, 0.03672923, -0.00025450048, -8.666277e-06)))
MESH = pl.DeviceIdType.MESH
VM = pl.BlockSpec(memory_space=pltpu.VMEM)
SM = pl.BlockSpec(memory_space=pltpu.SMEM)
ANY = pl.BlockSpec(memory_space=pl.ANY)


def audio_kernel(waves, first, mid, last, bias_in, out, weights, taps, bias,
                 stage, held, w, t32, t16, ssem, rsem, wsem, osem):
    f32, bf16 = jnp.float32, jnp.bfloat16
    dp, seq = lax.axis_index("dp"), lax.axis_index("seq")
    mine = seq == dp // 2
    barrier = pltpu.get_barrier_semaphore()

    def source(k):
        return {"dp": 4 * (seq // 2) + k, "seq": dp // 2}

    for k in range(4):
        @pl.when(jnp.logical_not(jnp.logical_and(mine, dp % 4 == k)))
        def _():
            pl.semaphore_signal(barrier, inc=1, device_id=source(k), device_id_type=MESH)

    def fetch(b):
        src = mid.at[pl.ds(1024 * b, 1024)] if b < 6 else last.at[pl.ds(1024 * (b - 6), 1024)]
        return pltpu.make_async_copy(src, w.at[pl.ds(1024 * b, 1024)], wsem.at[b])

    def leave(b):
        at = pl.ds(1024 * b, 1024)
        return pltpu.make_async_copy(w.at[at], weights.at[at], osem.at[b])

    for b in range(8):
        fetch(b).start()

    def unfold(i, _):
        for e in range(2):
            stage[e, pl.ds(i, 1), :] = waves[e:e + 1, pl.ds(pl.multiple_of(128 * i, 128), 128)]
        return 0
    lax.fori_loop(0, 320, unfold, 0, unroll=8)
    held[...] = stage[...].astype(bf16)
    pl.semaphore_wait(barrier, jnp.where(mine, 3, 4))
    slot = dp % 4

    def copy(e, c):
        return pltpu.make_async_remote_copy(
            src_ref=held.at[e], dst_ref=out.at[slot],
            send_sem=ssem.at[2 * e + c], recv_sem=rsem.at[slot],
            device_id={"dp": 2 * seq + e, "seq": 2 * (dp // 4) + c}, device_id_type=MESH)

    def here(e, c):
        return jnp.logical_and(mine, jnp.logical_and(dp % 2 == e, seq % 2 == c))

    def local(e, c):
        return pltpu.make_async_copy(held.at[e], out.at[slot], ssem.at[2 * e + c])

    for e in range(2):
        for c in range(2):
            @pl.when(jnp.logical_not(here(e, c)))
            def _():
                copy(e, c).start()

            @pl.when(here(e, c))
            def _():
                local(e, c).start()

    b0 = bias_in[...] - jnp.mean(bias_in[...], axis=-1, keepdims=True)
    bias[...] = b0
    fw = first[...] - jnp.mean(first[...], axis=-1, keepdims=True)
    hi = b0[0:1].astype(bf16).astype(f32)
    t32[...] = jnp.zeros_like(t32)
    for v in range(8):
        t32[v, 5 * v:5 * v + 10, :] = fw
        t32[v, 126:127, :] = hi
        t32[v, 127:128, :] = b0[0:1] - hi
    t16[...] = t32[...].astype(bf16)
    pltpu.make_async_copy(t16, taps, osem.at[8]).start()
    for b in range(8):
        fetch(b).wait()

        def centre(i, _):
            at = pl.ds(pl.multiple_of(1024 * b + 16 * i, 16), 16)
            x = w[at, :].astype(f32)
            w[at, :] = (x - jnp.mean(x, axis=-1, keepdims=True)).astype(bf16)
            return 0
        lax.fori_loop(0, 64, centre, 0, unroll=4)
        leave(b).start()

    for k in range(4):
        @pl.when(jnp.logical_not(jnp.logical_and(mine, slot == k)))
        def _():
            pltpu.make_async_remote_copy(
                src_ref=held.at[0], dst_ref=out.at[k], send_sem=ssem.at[0], recv_sem=rsem.at[k],
                device_id=source(k), device_id_type=MESH).wait_recv()
    for e in range(2):
        for c in range(2):
            @pl.when(jnp.logical_not(here(e, c)))
            def _():
                copy(e, c).wait_send()

            @pl.when(here(e, c))
            def _():
                local(e, c).wait()
    pltpu.make_async_copy(t16, taps, osem.at[8]).wait()
    for b in range(8):
        leave(b).wait()


def exchange_audio(waves, first, mid, last, bias):
    bf16, f32 = jnp.bfloat16, jnp.float32
    return pl.pallas_call(
        audio_kernel,
        out_shape=(jax.ShapeDtypeStruct((4, 320, 128), bf16), jax.ShapeDtypeStruct((8192, 512), bf16),
                   jax.ShapeDtypeStruct((8, 128, 512), bf16), jax.ShapeDtypeStruct((7, 512), f32)),
        in_specs=[VM, VM, ANY, ANY, VM],
        out_specs=(ANY, ANY, ANY, VM),
        scratch_shapes=[
            pltpu.VMEM((2, 320, 128), f32),
            pltpu.VMEM((2, 320, 128), bf16),
            pltpu.VMEM((8192, 512), bf16),
            pltpu.VMEM((8, 128, 512), f32),
            pltpu.VMEM((8, 128, 512), bf16),
            pltpu.SemaphoreType.DMA((4,)),
            pltpu.SemaphoreType.DMA((4,)),
            pltpu.SemaphoreType.DMA((8,)),
            pltpu.SemaphoreType.DMA((9,)),
        ],
        compiler_params=pltpu.CompilerParams(collective_id=1, has_side_effects=True, vmem_limit_bytes=24 << 20),
        name="audio",
    )(waves, first, mid.reshape(6144, 512), last.reshape(2048, 512), bias)


def half_gelu(h):
    h = h.astype(jnp.bfloat16)
    u = jnp.minimum(h * h, jnp.bfloat16(6.25))
    q = jnp.bfloat16(QH[3])
    for c in QH[2::-1]:
        q = q * u + jnp.bfloat16(c)
    return h + h * jnp.tanh(h * q)


def finish(v, gain, shift):
    ss = jnp.sum(v * v, axis=-1, keepdims=True)
    r = lax.rsqrt(ss * (1.0 / 512) + EPS)
    return half_gelu((v * r) * gain + shift)


def encoder_kernel(lens, order, utts_in, taps_in, w_in, bias, gain, shift, pgain, pshift, out,
                   utts, taps, w, packed, lhs, y0, y1, e1, e2, e3, e4, e5, e6, halo, out32, sem):
    f32, bf16 = jnp.float32, jnp.bfloat16
    seq = lax.axis_index("seq")
    own, core = seq // 2, seq % 2
    bounds = (0, 1536, 3072, 4608, 6144, 7168, 8192)

    def fetch(k):
        if k == 0:
            return pltpu.make_async_copy(utts_in, utts, sem.at[0])
        if k == 1:
            return pltpu.make_async_copy(taps_in, taps, sem.at[1])
        at = pl.ds(bounds[k - 2], bounds[k - 1] - bounds[k - 2])
        return pltpu.make_async_copy(w_in.at[at], w.at[at], sem.at[k])

    for k in range(8):
        fetch(k).start()
    packed[...] = jnp.zeros_like(packed)
    lane = lax.broadcasted_iota(jnp.int32, (320, 128), 1)
    sample = lax.broadcasted_iota(jnp.int32, (320, 128), 0) * 128 + lane
    fetch(0).wait()
    off = jnp.int32(0)
    for p in range(4):
        u = order[own, p]
        ln = lens[own, u]
        a, b = off // 128, off % 128
        part = jnp.where(sample < ln, utts[u].astype(f32), 0.0)
        rolled = pltpu.roll(part, b, 1)
        packed[pl.ds(a, 320), :] += jnp.where(lane >= b, rolled, 0.0)
        packed[pl.ds(a + 1, 320), :] += jnp.where(lane < b, rolled, 0.0)
        off = off + ln
    nv = ((off + 10239) // 10240 - core + 1) // 2

    def row(ref, l):
        return ref[pl.ds(l, 1), :]

    def dot_(a, b):
        return jnp.dot(a, b, preferred_element_type=f32)

    def epi(y, l, groups, dst):
        g, s = row(gain, l) * 0.5, row(shift, l) * 0.5
        b = row(bias, l)
        for k in range(groups):
            v = y[pl.ds(16 * k, 16), :]
            if l > 0:
                v = v + b
            dst(k, finish(v, g, s))

    def conv3(src, l, start, rows, gap, y):
        at = 1536 * l
        y[pl.ds(0, rows), :] = dot_(src[pl.ds(start, rows), :], w[at:at + 1024, :]) + dot_(
            src[pl.ds(start + gap, rows), 0:512], w[at + 1024:at + 1536, :])

    def put(ref, gap, base=0):
        def at(k, v):
            ref[pl.ds((k // 2) * gap + base, 16), (k % 2) * 512:(k % 2) * 512 + 512] = v
        return at

    lane16 = lax.broadcasted_iota(jnp.int32, (16, 128), 1)
    row16 = lax.broadcasted_iota(jnp.int32, (16, 512), 0)

    def windows(cols, count):
        for q in range(count):
            j, o = divmod(40 * q, 128)
            x = cols[j] if o == 0 else pltpu.roll(cols[j], 128 - o, 1)
            if o + 45 > 128:
                x = jnp.where(lane16 < 128 - o, x, pltpu.roll(cols[j + 1], 128 - o, 1))
            x = jnp.where(lane16 >= 126, 1.0, x)
            lhs[pl.ds(16 * q, 16), :] = x.astype(bf16)

    after = packed[pl.ds(80 * core + 80, 8, stride=160), :]
    windows([jnp.concatenate([after, jnp.zeros((8, 128), f32)], axis=0)], 2)
    fetch(1).wait()
    for v in range(8):
        y0[pl.ds(32 * v, 32), :] = dot_(lhs[0:32, :], taps[v])

    def put_first(k, val):
        ph = 8 * (k % 2) + k // 2
        e1[pl.ds(16 * (ph // 2), 16), (ph % 2) * 512:(ph % 2) * 512 + 512] = val
    epi(y0, 0, 16, put_first)
    fetch(2).wait()
    conv3(e1, 0, 0, 112, 16, y0)
    epi(y0, 1, 7, put(e2, 16))
    fetch(3).wait()
    conv3(e2, 1, 0, 48, 16, y0)
    epi(y0, 2, 3, put(e3, 16))
    fetch(4).wait()
    conv3(e3, 2, 0, 16, 16, y0)

    def keep4(k, val):
        halo[48:64, :] = val.astype(f32)
    epi(y0, 3, 1, keep4)
    for k, e in enumerate((e1, e2, e3)):
        halo[16 * k:16 * k + 16, :] = e[0:16, 0:512].astype(f32)
    silent = jnp.broadcast_to(halo[56:57, :], (16, 512)).astype(bf16)

    def fill(i, _):
        for k in range(17):
            e4[pl.ds((k // 2) * 128 + 16 * i, 16), (k % 2) * 512:(k % 2) * 512 + 512] = silent
        return 0
    lax.fori_loop(nv, 8, fill, 0)

    def wrap(e, l, i, first, last):
        x = pltpu.roll(e[pl.ds(first, 16), 0:512].astype(f32), 15, 0)
        x = jnp.where(row16 == 15, halo[pl.ds(16 * l + i, 1), :], x)
        e[pl.ds(last, 16), 0:512] = x.astype(bf16)

    def segment(i, _):
        base = 5 * (32 * i + 16 * core)
        windows([packed[pl.ds(base + j, 16, stride=5), :] for j in range(6)], 16)

        def first(v, y):
            y[...] = dot_(lhs[...], taps[v])

        def put1(v):
            def at(q, val):
                e1[pl.ds(64 * q + 16 * (v // 2), 16), 512 * (v % 2):512 * (v % 2) + 512] = val
            return at
        ys = (y0, y1)
        first(0, y0)
        for v in range(8):
            if v < 7:
                first(v + 1, ys[(v + 1) % 2])
            epi(ys[v % 2], 0, 16, put1(v))
        wrap(e1, 0, i, 0, 1024)
        conv3(e1, 0, 0, 256, 16, y0)
        conv3(e1, 0, 256, 256, 16, y1)
        epi(y0, 1, 16, put(e2, 16, 0))
        conv3(e1, 0, 512, 256, 16, y0)
        epi(y1, 1, 16, put(e2, 16, 128))
        conv3(e1, 0, 768, 256, 16, y1)
        epi(y0, 1, 16, put(e2, 16, 256))
        conv3(e2, 1, 0, 256, 16, y0)
        epi(y1, 1, 16, put(e2, 16, 384))
        wrap(e2, 1, i, 0, 512)
        conv3(e2, 1, 256, 256, 16, y1)
        epi(y0, 2, 16, put(e3, 16, 0))
        epi(y1, 2, 16, put(e3, 16, 128))
        wrap(e3, 2, i, 0, 256)
        conv3(e3, 2, 0, 256, 16, y0)
        at = pl.multiple_of(16 * i, 16)
        epi(y0, 3, 16, put(e4, 128, at))
        wrap(e4, 3, i, at, 1024 + at)
        return 0
    lax.fori_loop(0, nv, segment, 0)
    for k in range(5, 8):
        fetch(k).wait()

    def conv2(src, l, start, y):
        y[...] = dot_(src[pl.ds(start, 256), :], w[6144 + 1024 * l:7168 + 1024 * l, :])

    def put8(ref, base):
        def at(k, v):
            ref[pl.ds(base + 16 * (k % 8), 16), (k // 8) * 512:(k // 8) * 512 + 512] = v
        return at
    conv3(e4, 3, 0, 256, 128, y0)
    conv3(e4, 3, 256, 256, 128, y1)
    epi(y0, 4, 16, put8(e5, 0))
    conv3(e4, 3, 512, 256, 128, y0)
    epi(y1, 4, 16, put8(e5, 128))
    conv3(e4, 3, 768, 256, 128, y1)
    epi(y0, 4, 16, put8(e5, 256))
    conv2(e5, 0, 0, y0)
    epi(y1, 4, 16, put8(e5, 384))
    conv2(e5, 0, 256, y1)
    epi(y0, 5, 16, put8(e6, 0))
    epi(y1, 5, 16, put8(e6, 128))
    conv2(e6, 1, 0, y0)
    pg, ps = pgain[...], pshift[...]

    def last(k, v):
        v = v.astype(f32)
        v = v - jnp.mean(v, axis=-1, keepdims=True)
        v = v * lax.rsqrt(jnp.mean(v * v, axis=-1, keepdims=True) + EPS) * pg + ps
        for c in range(4):
            out32[c, pl.ds(32 * (k % 8) + k // 8, 16, stride=2), :] = v[:, 128 * c:128 * c + 128]
    epi(y0, 6, 16, last)
    out[0:32, :] = jnp.zeros((32, 512), bf16)
    out[288:320, :] = jnp.zeros((32, 512), bf16)
    for c in range(4):
        out[32:288, 128 * c:128 * c + 128] = out32[c].astype(bf16)


def encode(lens, order, utts, taps, weights, bias, gain, shift, pgain, pshift):
    bf16, f32 = jnp.bfloat16, jnp.float32
    return pl.pallas_call(
        encoder_kernel,
        out_shape=jax.ShapeDtypeStruct((320, 512), bf16),
        in_specs=[SM, SM, ANY, ANY, ANY] + [VM] * 5,
        out_specs=VM,
        scratch_shapes=[
            pltpu.VMEM((4, 320, 128), bf16),
            pltpu.VMEM((8, 128, 512), bf16),
            pltpu.VMEM((8192, 512), bf16),
            pltpu.VMEM((1296, 128), f32),
            pltpu.VMEM((256, 128), bf16),
            pltpu.VMEM((256, 512), f32),
            pltpu.VMEM((256, 512), f32),
            pltpu.VMEM((65 * 16, 1024), bf16),
            pltpu.VMEM((33 * 16, 1024), bf16),
            pltpu.VMEM((17 * 16, 1024), bf16),
            pltpu.VMEM((9 * 128, 1024), bf16),
            pltpu.VMEM((4 * 128, 1024), bf16),
            pltpu.VMEM((2 * 128, 1024), bf16),
            pltpu.VMEM((64, 512), f32),
            pltpu.VMEM((4, 256, 128), f32),
            pltpu.SemaphoreType.DMA((8,)),
        ],
        compiler_params=pltpu.CompilerParams(vmem_limit_bytes=40 << 20),
        name="encode",
    )(lens, order, utts, taps, weights, bias, gain, shift, pgain, pshift)


def frames_kernel(frames, out, ssem, rsem):
    seq = lax.axis_index("seq")
    barrier = pltpu.get_barrier_semaphore()
    for o in range(1, 8):
        pl.semaphore_signal(barrier, inc=1, device_id={"seq": (seq + o) % 8}, device_id_type=MESH)

    def piece(d):
        return frames.at[pl.ds(pl.multiple_of(32 * d + 32 * (1 - seq % 2), 32), 64)]

    def copy(o):
        d = (seq + o) % 8
        return pltpu.make_async_remote_copy(
            src_ref=piece(d), dst_ref=out.at[seq], send_sem=ssem.at[o], recv_sem=rsem.at[seq],
            device_id={"seq": d}, device_id_type=MESH)
    own = pltpu.make_async_copy(piece(seq), out.at[seq], ssem.at[0])
    own.start()
    pl.semaphore_wait(barrier, 7)
    for o in range(1, 8):
        copy(o).start()
    own.wait()
    for o in range(1, 8):
        d = (seq + o) % 8
        pltpu.make_async_remote_copy(
            src_ref=piece(d), dst_ref=out.at[d], send_sem=ssem.at[o], recv_sem=rsem.at[d],
            device_id={"seq": d}, device_id_type=MESH).wait_recv()
    for o in range(1, 8):
        copy(o).wait_send()


def exchange_frames(frames):
    return pl.pallas_call(
        frames_kernel,
        out_shape=jax.ShapeDtypeStruct((8, 64, 512), jnp.bfloat16),
        in_specs=[ANY],
        out_specs=ANY,
        scratch_shapes=[pltpu.SemaphoreType.DMA((8,)), pltpu.SemaphoreType.DMA((8,))],
        compiler_params=pltpu.CompilerParams(collective_id=2, has_side_effects=True, vmem_limit_bytes=1 << 20),
        name="frames",
    )(frames)


def conformer_kernel(lens, recv_in, wp_in, pb, gain, up_in, taps, dbias, down_in, out,
                     recv, wp, up, down, nrm, s0, s1, lifted, ya, yb, g, act, sem):
    f32, bf16 = jnp.float32, jnp.bfloat16
    pairs = ((recv_in, recv), (wp_in, wp), (up_in.at[0], up.at[0]), (down_in.at[0], down.at[0]),
             (up_in.at[1], up.at[1]), (down_in.at[1], down.at[1]))

    def fetch(k):
        return pltpu.make_async_copy(pairs[k][0], pairs[k][1], sem.at[k])
    for k in range(6):
        fetch(k).start()
    fetch(0).wait()
    base = 64 * lax.axis_index("seq") - 32
    for r in range(4):
        for c in range(4):
            nrm[128 * r + 32 * c:128 * r + 32 * c + 32, :] = recv[2 * r + (c + 1) % 2, 32 * (c // 2):32 * (c // 2) + 32, :]

    def dot_(a, b):
        return jnp.dot(a, b, preferred_element_type=f32)

    fetch(1).wait()
    for n in range(4):
        w = slice(256 * n, 256 * n + 256)
        s0[:, w] = dot_(nrm[...], wp[:, w]) + pb[:, w]

    def norm(src, l, rows):
        gl = gain[l:l + 1, :]

        def body(i, _):
            at = pl.ds(pl.multiple_of(16 * i, 16), 16)
            v = src[at, :]
            v = v - jnp.mean(v, axis=-1, keepdims=True)
            v = v * lax.rsqrt(jnp.mean(v * v, axis=-1, keepdims=True) + EPS) * gl
            lifted[at, :] = v.astype(bf16)
            return 0
        lax.fori_loop(0, rows // 16, body, 0, unroll=2)

    def module(l, per, lo, keep):
        rows = 4 * per

        def chunk(n, _):
            wa = pl.ds(pl.multiple_of(256 * n, 256), 256)
            wb = pl.ds(pl.multiple_of(1024 + 256 * n, 256), 256)
            ya[0:rows, :] = dot_(lifted[0:rows, :], up[l, :, wa])
            yb[0:rows, :] = dot_(lifted[0:rows, :], up[l, :, wb])
            for r in range(4):
                total = lens[r, 0] + lens[r, 1] + lens[r, 2] + lens[r, 3]
                valid = (total - 400) // 320 + 1
                for k in range(per // 16):
                    at = slice(per * r + 16 * k, per * r + 16 * k + 16)
                    t = base + lo + 16 * k + lax.broadcasted_iota(jnp.int32, (16, 256), 0)
                    live = jnp.logical_and(t >= 0, t < valid)
                    v = jnp.where(live, ya[at, :] * jax.nn.sigmoid(yb[at, :]), 0.0)
                    g[2 * n, r, lo + 16 * k:lo + 16 * k + 16, :] = v[:, 0:128]
                    g[2 * n + 1, r, lo + 16 * k:lo + 16 * k + 16, :] = v[:, 128:256]
            return 0
        lax.fori_loop(0, 4, chunk, 0)
        first = 64 - keep // 2

        def depth(c, _):
            w = pl.ds(pl.multiple_of(128 * c, 128), 128)

            def one(r, _):
                acc = jnp.broadcast_to(dbias[l:l + 1, w], (keep, 128))
                for j in range(31):
                    acc = acc + g[c, r, first + j - 15:first + j - 15 + keep, :] * taps[j, l:l + 1, w]
                act[pl.ds(pl.multiple_of(keep * r, 32), keep), w] = (acc * jax.nn.sigmoid(acc)).astype(bf16)
                return 0
            return lax.fori_loop(0, 4, one, 0)
        lax.fori_loop(0, 8, depth, 0)

    norm(s0, 0, 512)
    fetch(2).wait()
    module(0, 128, 0, 96)
    fetch(3).wait()
    for n in range(4):
        w = slice(256 * n, 256 * n + 256)
        d = dot_(act[...], down[0, :, w])
        for r in range(4):
            s1[96 * r:96 * r + 96, w] = s0[128 * r + 16:128 * r + 112, w] + d[96 * r:96 * r + 96]
    norm(s1, 1, 384)
    fetch(4).wait()
    module(1, 96, 16, 64)
    fetch(5).wait()
    for n in range(4):
        w = slice(256 * n, 256 * n + 256)
        d = dot_(act[0:256, :], down[1, :, w])
        for r in range(4):
            out[r, :, w] = (s1[96 * r + 16:96 * r + 80, w] + d[64 * r:64 * r + 64]).astype(bf16)


def conform(lens, recv, wp, pb, gain, up, taps, dbias, down):
    bf16, f32 = jnp.bfloat16, jnp.float32
    return pl.pallas_call(
        conformer_kernel,
        out_shape=jax.ShapeDtypeStruct((4, 64, 1024), bf16),
        in_specs=[SM, ANY, ANY, VM, VM, ANY, VM, VM, ANY],
        out_specs=VM,
        scratch_shapes=[
            pltpu.VMEM((8, 64, 512), bf16),
            pltpu.VMEM((512, 1024), bf16),
            pltpu.VMEM((2, 1024, 2048), bf16),
            pltpu.VMEM((2, 1024, 1024), bf16),
            pltpu.VMEM((512, 512), bf16),
            pltpu.VMEM((512, 1024), f32),
            pltpu.VMEM((384, 1024), f32),
            pltpu.VMEM((512, 1024), bf16),
            pltpu.VMEM((512, 256), f32),
            pltpu.VMEM((512, 256), f32),
            pltpu.VMEM((8, 4, 128, 128), f32),
            pltpu.VMEM((384, 1024), bf16),
            pltpu.SemaphoreType.DMA((6,)),
        ],
        compiler_params=pltpu.CompilerParams(vmem_limit_bytes=40 << 20),
        name="conform",
    )(lens, recv, wp, pb, gain, up, jnp.transpose(taps, (1, 0, 2)), dbias, down)


def per_device(waveforms, utt_len, pack_order, conv_first, conv_mid, conv_last, conv_bias, conv_gain,
               conv_shift, proj_gain, proj_shift, proj_weight, proj_bias, conf_gain, conf_up,
               conf_depth, depth_bias, conf_down):
    utts, weights, taps, bias = exchange_audio(waveforms, conv_first, conv_mid, conv_last, conv_bias)
    frames = encode(utt_len, pack_order, utts, taps, weights, bias, conv_gain, conv_shift,
                    proj_gain[None], proj_shift[None])
    recv = exchange_frames(frames)
    return conform(utt_len, recv, proj_weight, proj_bias[None], conf_gain, conf_up, conf_depth,
                   depth_bias, conf_down)


def solution(mesh):
    return jax.shard_map(
        per_device,
        mesh=mesh,
        in_specs=(P(("dp", "seq"), None), P("dp", None), P("dp", None)) + (P(),) * 15,
        out_specs=P("dp", "seq", None),
        check_vma=False,
    )
```

time: 147 us -> 140 us (0.952)
  the two profiles are of different devices: /device:TPU:71 before, /device:TPU:7 now
where the time goes in v1:
time: 140 us
  Pallas kernels  126 us (90%)
  local copies, waits for them, and re-layouts  13.5 us (10%)
    pallas_call x1, Pallas kernels, exchange_audio(): pl.pallas_call(audio_kernel, out_shape=(jax.ShapeDtypeStruct((4, 320, 128...  51.3 us
    pallas_call x1, Pallas kernels, encode(): pl.pallas_call(encoder_kernel, out_shape=jax.ShapeDtypeStruct((320, 512),...  31.1 us
    pallas_call x1, Pallas kernels, conform(): pl.pallas_call(conformer_kernel, out_shape=jax.ShapeDtypeStruct((4, 64, 1...  22.5 us
    pallas_call x1, Pallas kernels, exchange_frames(): pl.pallas_call(frames_kernel, out_shape=jax.ShapeDtypeStruct((8, 64, 512)...  20.9 us
    unnamed x42, local copies, waits for them, and re-layouts  13.5 us

profile of v1, /device:TPU:7, one launch (start us, length us, event | category | flops | bytes accessed | tf_op | source)
XLA Modules:
  0.0 139.7 jit_solution(1658600545810699372)
XLA Ops:
  0.0 0.0 copy-start.14
  0.0 0.0 copy-start.18
  0.0 0.0 copy-start.17
  0.0 0.0 copy-start.16
  0.0 0.0 copy-start.2
  0.0 2.8 %copy-done.2 = bf16[4,3,512,512]{3,2,1,0:T(8,128)(2,1)S(1)} copy-done((bf16[4,3,512,512]{3,2,1,0:T(8,128)(2,1)S(1)}, bf16[4,3,512,512]{3,2,1,0:T(8,128)(2,1)}, u32[]{:S(2)}) %copy-start.2) | copy-done | bytes 6291480
  2.8 0.0 copy-start.4
  2.9 1.6 %copy-done.4 = bf16[2,2,512,512]{3,2,1,0:T(8,128)(2,1)S(1)} copy-done((bf16[2,2,512,512]{3,2,1,0:T(8,128)(2,1)S(1)}, bf16[2,2,512,512]{3,2,1,0:T(8,128)(2,1)}, u32[]{:S(2)}) %copy-start.4) | copy-done | bytes 2097176
  4.4 0.0 copy-start.6
  4.4 1.0 copy-done.6
  5.4 0.0 copy-start.8
  5.4 0.8 copy-done.8
  6.2 0.0 copy-start.9
  6.2 0.7 copy-done.9
  6.9 0.0 copy-start.10
  6.9 0.0 copy-start.11
  6.9 0.0 slice-start
  6.9 0.0 copy-start.3
  6.9 0.0 copy-start.7
  6.9 0.0 copy-start.12
  6.9 0.0 copy-start.13
  6.9 51.3 %audio.1 = (bf16[4,320,128]{2,1,0:T(8,128)(2,1)S(1)}, bf16[8192,512]{1,0:T(8,128)(2,1)S(1)}, bf16[8,128,512]{2,1,0:T(8,128)(2,1)S(1)}, f32[7,512]{1,0:T(8,128)S(1)}) custom-call(f32[2,40960]{1,0:T(2,128)S(1)} %copy-done.6, f32[10,512]{1,0:T(8,128)S(1)} %copy-done.8, bf16[6144,512]{1,0:T(8,128)(2,1)S(1)} %bitcast.8, bf16[2048,512]{1,0:T(8,128)(2,1)S(1)} %bitcast.9, ...), custom_call_target="tpu_custom_call" | custom-call | tf_op jit(solution)/shard_map/audio/pallas_call | solution.py:117
  58.2 0.0 copy-start
  58.2 3.2 %copy-done = bf16[8192,512]{1,0:T(8,128)(2,1)} copy-done((bf16[8192,512]{1,0:T(8,128)(2,1)}, bf16[8192,512]{1,0:T(8,128)(2,1)S(1)}, u32[]{:S(2)}) %copy-start) | copy-done | bytes 8388632
  61.5 0.0 copy-start.15
  61.5 0.0 copy-done.14
  61.5 0.0 copy-done.18
  61.5 0.0 copy-done.17
  61.5 0.0 copy-done.16
  61.5 0.0 copy-done.10
  61.5 0.0 copy-done.11
  61.5 0.0 copy-start.1
  61.5 3.4 %copy-done.1 = bf16[8192,512]{1,0:T(8,128)(2,1)S(1)} copy-done((bf16[8192,512]{1,0:T(8,128)(2,1)S(1)}, bf16[8192,512]{1,0:T(8,128)(2,1)}, u32[]{:S(2)}) %copy-start.1) | copy-done | bytes 8388632
  64.9 0.0 slice-start.1
  64.9 0.0 copy-start.5
  64.9 31.1 %encode.1.frames = bf16[320,512]{1,0:T(8,128)(2,1)S(1)} custom-call(s32[4,4]{1,0:T(4,128)S(1)} %copy-done.14, s32[4,4]{1,0:T(4,128)S(1)} %copy-done.16, bf16[4,320,128]{2,1,0:T(8,128)(2,1)S(1)} %get-tuple-element.9.utts_in, bf16[8,128,512]{2,1,0:T(8,128)(2,1)S(1)} %get-tuple-element.10.taps_in, bf16[8192,512]{1,0:T(8,128)(2,1)S(1)} %copy-done.1, ...), custom_call_target="tpu_custom_call" | custom-call | tf_op jit(solution)/shard_map/encode/pallas_call | solution.py:339
  96.0 20.9 %frames.1.recv_in = bf16[8,64,512]{2,1,0:T(8,128)(2,1)S(1)} custom-call(bf16[320,512]{1,0:T(8,128)(2,1)S(1)} %encode.1.frames), custom_call_target="tpu_custom_call" | custom-call | tf_op jit(solution)/shard_map/frames/pallas_call | solution.py:397
  117.0 0.0 slice-done
  117.0 0.0 copy-done.3
  117.0 0.0 copy-done.7
  117.0 0.0 copy-done.12
  117.0 0.0 copy-done.13
  117.0 0.0 copy-done.15
  117.0 0.0 slice-done.1
  117.0 0.0 copy-done.5
  117.1 22.5 %conform.1 = bf16[4,64,1024]{2,1,0:T(8,128)(2,1)} custom-call(s32[4,4]{1,0:T(4,128)S(1)} %copy-done.14, bf16[8,64,512]{2,1,0:T(8,128)(2,1)S(1)} %frames.1.recv_in, bf16[512,1024]{1,0:T(8,128)(2,1)S(1)} %copy-done.5, f32[1,1024]{1,0:T(1,128)S(1)} %bitcast.11, f32[2,1024]{1,0:T(2,128)S(1)} %copy-done.12, bf16[2,1024,2048]{2,1,0:T(8,128)(2,1)S(1)} %bitcast.7, ...), custom_call_target="tpu_custom_call" | custom-call | tf_op jit(solution)/shard_map/conform/pallas_call | solution.py:500
  (1 shorter events, 0.0 us)
Async XLA Ops:
  0.0 61.5 %copy-start.14 = (s32[4,4]{1,0:T(4,128)S(1)}, s32[4,4]{1,0:T(4,128)}, u32[]{:S(2)}) copy-start(s32[4,4]{1,0:T(4,128)} %lens.3) | copy-start | bytes 196
  0.0 61.5 %copy-start.18 = (f32[512]{0:T(512)S(1)}, f32[512]{0:T(512)}, u32[]{:S(2)}) copy-start(f32[512]{0:T(512)} %param.28) | copy-start | bytes 6148
  0.0 61.5 %copy-start.17 = (f32[512]{0:T(512)S(1)}, f32[512]{0:T(512)}, u32[]{:S(2)}) copy-start(f32[512]{0:T(512)} %param.27) | copy-start | bytes 6148
  0.0 61.5 %copy-start.16 = (s32[4,4]{1,0:T(4,128)S(1)}, s32[4,4]{1,0:T(4,128)}, u32[]{:S(2)}) copy-start(s32[4,4]{1,0:T(4,128)} %order.1) | copy-start | bytes 196
  0.0 2.8 %copy-start.2 = (bf16[4,3,512,512]{3,2,1,0:T(8,128)(2,1)S(1)}, bf16[4,3,512,512]{3,2,1,0:T(8,128)(2,1)}, u32[]{:S(2)}) copy-start(bf16[4,3,512,512]{3,2,1,0:T(8,128)(2,1)} %param.22) | copy-start | bytes 18874372
  2.8 1.6 %copy-start.4 = (bf16[2,2,512,512]{3,2,1,0:T(8,128)(2,1)S(1)}, bf16[2,2,512,512]{3,2,1,0:T(8,128)(2,1)}, u32[]{:S(2)}) copy-start(bf16[2,2,512,512]{3,2,1,0:T(8,128)(2,1)} %param.23) | copy-start | bytes 6291460
  4.4 1.0 copy-start.6
  5.4 0.8 copy-start.8
  6.2 0.7 copy-start.9
  6.9 54.6 %copy-start.10 = (f32[7,512]{1,0:T(8,128)S(1)}, f32[7,512]{1,0:T(8,128)}, u32[]{:S(2)}) copy-start(f32[7,512]{1,0:T(8,128)} %gain.2) | copy-start | bytes 43012
  6.9 54.6 %copy-start.11 = (f32[7,512]{1,0:T(8,128)S(1)}, f32[7,512]{1,0:T(8,128)}, u32[]{:S(2)}) copy-start(f32[7,512]{1,0:T(8,128)} %shift.1) | copy-start | bytes 43012
  6.9 110.1 %slice-start = ((s8[8388608]{0:T(1024)(128)(4,1)}), s8[4194304]{0:T(1024)(128)(4,1)S(1)}, s32[]{:S(2)}) async-start(s8[8388608]{0:T(1024)(128)(4,1)} %bitcast.6), calls=%async_computation | async-start | bytes 8388608
  6.9 110.1 %copy-start.3 = (bf16[2,1024,1024]{2,1,0:T(8,128)(2,1)S(1)}, bf16[2,1024,1024]{2,1,0:T(8,128)(2,1)}, u32[]{:S(2)}) copy-start(bf16[2,1024,1024]{2,1,0:T(8,128)(2,1)} %down_in.1) | copy-start | bytes 12582916
  6.9 110.1 %copy-start.7 = (f32[2,31,1024]{2,0,1:T(2,128)S(1)}, f32[2,31,1024]{2,0,1:T(2,128)}, u32[]{:S(2)}) copy-start(f32[2,31,1024]{2,0,1:T(2,128)} %param.33) | copy-start | bytes 761860
  6.9 110.1 %copy-start.12 = (f32[2,1024]{1,0:T(2,128)S(1)}, f32[2,1024]{1,0:T(2,128)}, u32[]{:S(2)}) copy-start(f32[2,1024]{1,0:T(2,128)} %gain.3) | copy-start | bytes 24580
  6.9 110.1 %copy-start.13 = (f32[2,1024]{1,0:T(2,128)S(1)}, f32[2,1024]{1,0:T(2,128)}, u32[]{:S(2)}) copy-start(f32[2,1024]{1,0:T(2,128)} %dbias.1) | copy-start | bytes 24580
  58.2 3.3 %copy-start = (bf16[8192,512]{1,0:T(8,128)(2,1)}, bf16[8192,512]{1,0:T(8,128)(2,1)S(1)}, u32[]{:S(2)}) copy-start(bf16[8192,512]{1,0:T(8,128)(2,1)S(1)} %get-tuple-element.11.w_in) | copy-start | bytes 25165828
  61.5 55.6 %copy-start.15 = (f32[1024]{0:T(1024)S(1)}, f32[1024]{0:T(1024)}, u32[]{:S(2)}) copy-start(f32[1024]{0:T(1024)} %param.30) | copy-start | bytes 12292
  61.5 3.4 %copy-start.1 = (bf16[8192,512]{1,0:T(8,128)(2,1)S(1)}, bf16[8192,512]{1,0:T(8,128)(2,1)}, u32[]{:S(2)}) copy-start(bf16[8192,512]{1,0:T(8,128)(2,1)} %copy-done) | copy-start | bytes 25165828
  64.9 52.1 %slice-start.1 = ((s8[8388608]{0:T(1024)(128)(4,1)}), s8[4194304]{0:T(1024)(128)(4,1)S(1)}, s32[]{:S(2)}) async-start(s8[8388608]{0:T(1024)(128)(4,1)} %bitcast.6), calls=%async_computation.1 | async-start | bytes 8388608
  64.9 52.1 %copy-start.5 = (bf16[512,1024]{1,0:T(8,128)(2,1)S(1)}, bf16[512,1024]{1,0:T(8,128)(2,1)}, u32[]{:S(2)}) copy-start(bf16[512,1024]{1,0:T(8,128)(2,1)} %wp_in.1) | copy-start | bytes 3145732

commit v2 on v1

--- a/solution.py
+++ b/solution.py
@@ -11,10 +11,11 @@
 VM = pl.BlockSpec(memory_space=pltpu.VMEM)
 SM = pl.BlockSpec(memory_space=pltpu.SMEM)
 ANY = pl.BlockSpec(memory_space=pl.ANY)
-
-
-def audio_kernel(waves, first, mid, last, bias_in, out, weights, taps, bias,
-                 stage, held, w, t32, t16, ssem, rsem, wsem, osem):
+HBM = pl.BlockSpec(memory_space=pltpu.HBM)
+
+
+def audio_kernel(waves_in, first_in, mid, last, bias_in, out, weights, taps, bias,
+                 waves, first, bias_raw, stage, held, raw, w, means, t32, t16, ssem, rsem, wsem, osem):
     f32, bf16 = jnp.float32, jnp.bfloat16
     dp, seq = lax.axis_index("dp"), lax.axis_index("seq")
     mine = seq == dp // 2
@@ -30,14 +31,19 @@
 
     def fetch(b):
         src = mid.at[pl.ds(1024 * b, 1024)] if b < 6 else last.at[pl.ds(1024 * (b - 6), 1024)]
-        return pltpu.make_async_copy(src, w.at[pl.ds(1024 * b, 1024)], wsem.at[b])
+        return pltpu.make_async_copy(src, raw.at[pl.ds(1024 * b, 1024)], wsem.at[b])
 
     def leave(b):
         at = pl.ds(1024 * b, 1024)
         return pltpu.make_async_copy(w.at[at], weights.at[at], osem.at[b])
 
+    small = [pltpu.make_async_copy(x, y, wsem.at[8 + k]) for k, (x, y) in enumerate(
+        ((waves_in, waves), (first_in, first), (bias_in, bias_raw)))]
+    for c in small:
+        c.start()
     for b in range(8):
         fetch(b).start()
+    small[0].wait()
 
     def unfold(i, _):
         for e in range(2):
@@ -70,7 +76,9 @@
             def _():
                 local(e, c).start()
 
-    b0 = bias_in[...] - jnp.mean(bias_in[...], axis=-1, keepdims=True)
+    small[1].wait()
+    small[2].wait()
+    b0 = bias_raw[...] - jnp.mean(bias_raw[...], axis=-1, keepdims=True)
     bias[...] = b0
     fw = first[...] - jnp.mean(first[...], axis=-1, keepdims=True)
     hi = b0[0:1].astype(bf16).astype(f32)
@@ -81,15 +89,19 @@
         t32[v, 127:128, :] = b0[0:1] - hi
     t16[...] = t32[...].astype(bf16)
     pltpu.make_async_copy(t16, taps, osem.at[8]).start()
+    ones = jnp.full((512, 128), 1.0 / 512, bf16)
     for b in range(8):
         fetch(b).wait()
+        means[...] = jnp.dot(raw[1024 * b:1024 * b + 1024, :], ones, preferred_element_type=f32)
 
         def centre(i, _):
-            at = pl.ds(pl.multiple_of(1024 * b + 16 * i, 16), 16)
-            x = w[at, :].astype(f32)
-            w[at, :] = (x - jnp.mean(x, axis=-1, keepdims=True)).astype(bf16)
+            at = pl.ds(pl.multiple_of(1024 * b + 32 * i, 32), 32)
+            m = means[pl.ds(pl.multiple_of(32 * i, 32), 32), :]
+            for c in range(4):
+                k = slice(128 * c, 128 * c + 128)
+                w[at, k] = (raw[at, k].astype(f32) - m).astype(bf16)
             return 0
-        lax.fori_loop(0, 64, centre, 0, unroll=4)
+        lax.fori_loop(0, 32, centre, 0, unroll=4)
         leave(b).start()
 
     for k in range(4):
@@ -118,22 +130,28 @@
         audio_kernel,
         out_shape=(jax.ShapeDtypeStruct((4, 320, 128), bf16), jax.ShapeDtypeStruct((8192, 512), bf16),
                    jax.ShapeDtypeStruct((8, 128, 512), bf16), jax.ShapeDtypeStruct((7, 512), f32)),
-        in_specs=[VM, VM, ANY, ANY, VM],
-        out_specs=(ANY, ANY, ANY, VM),
+        in_specs=[HBM, HBM, HBM, HBM, HBM],
+        out_specs=(HBM, HBM, HBM, VM),
         scratch_shapes=[
+            pltpu.VMEM((2, 40960), f32),
+            pltpu.VMEM((10, 512), f32),
+            pltpu.VMEM((7, 512), f32),
             pltpu.VMEM((2, 320, 128), f32),
             pltpu.VMEM((2, 320, 128), bf16),
             pltpu.VMEM((8192, 512), bf16),
+            pltpu.VMEM((8192, 512), bf16),
+            pltpu.VMEM((1024, 128), f32),
             pltpu.VMEM((8, 128, 512), f32),
             pltpu.VMEM((8, 128, 512), bf16),
             pltpu.SemaphoreType.DMA((4,)),
             pltpu.SemaphoreType.DMA((4,)),
-            pltpu.SemaphoreType.DMA((8,)),
+            pltpu.SemaphoreType.DMA((11,)),
             pltpu.SemaphoreType.DMA((9,)),
         ],
-        compiler_params=pltpu.CompilerParams(collective_id=1, has_side_effects=True, vmem_limit_bytes=24 << 20),
+        compiler_params=pltpu.CompilerParams(collective_id=1, has_side_effects=True, vmem_limit_bytes=26 << 20),
         name="audio",
-    )(waves, first, mid.reshape(6144, 512), last.reshape(2048, 512), bias)
+    )(*[pltpu.with_memory_space_constraint(x, pltpu.HBM) for x in (
+        waves, first, mid.reshape(6144, 512), last.reshape(2048, 512), bias)])
 
 
 def half_gelu(h):
@@ -339,7 +357,7 @@
     return pl.pallas_call(
         encoder_kernel,
         out_shape=jax.ShapeDtypeStruct((320, 512), bf16),
-        in_specs=[SM, SM, ANY, ANY, ANY] + [VM] * 5,
+        in_specs=[SM, SM, HBM, HBM, HBM] + [VM] * 5,
         out_specs=VM,
         scratch_shapes=[
             pltpu.VMEM((4, 320, 128), bf16),
@@ -359,7 +377,7 @@
             pltpu.VMEM((4, 256, 128), f32),
             pltpu.SemaphoreType.DMA((8,)),
         ],
-        compiler_params=pltpu.CompilerParams(vmem_limit_bytes=40 << 20),
+        compiler_params=pltpu.CompilerParams(vmem_limit_bytes=30 << 20),
         name="encode",
     )(lens, order, utts, taps, weights, bias, gain, shift, pgain, pshift)
 
@@ -397,25 +415,17 @@
     return pl.pallas_call(
         frames_kernel,
         out_shape=jax.ShapeDtypeStruct((8, 64, 512), jnp.bfloat16),
-        in_specs=[ANY],
-        out_specs=ANY,
+        in_specs=[HBM],
+        out_specs=HBM,
         scratch_shapes=[pltpu.SemaphoreType.DMA((8,)), pltpu.SemaphoreType.DMA((8,))],
         compiler_params=pltpu.CompilerParams(collective_id=2, has_side_effects=True, vmem_limit_bytes=1 << 20),
         name="frames",
     )(frames)
 
 
-def conformer_kernel(lens, recv_in, wp_in, pb, gain, up_in, taps, dbias, down_in, out,
-                     recv, wp, up, down, nrm, s0, s1, lifted, ya, yb, g, act, sem):
+def conformer_kernel(lens, recv, wp, pb, gain, up, taps, dbias, down, out,
+                     nrm, s0, s1, lifted, ya, yb, g, act):
     f32, bf16 = jnp.float32, jnp.bfloat16
-    pairs = ((recv_in, recv), (wp_in, wp), (up_in.at[0], up.at[0]), (down_in.at[0], down.at[0]),
-             (up_in.at[1], up.at[1]), (down_in.at[1], down.at[1]))
-
-    def fetch(k):
-        return pltpu.make_async_copy(pairs[k][0], pairs[k][1], sem.at[k])
-    for k in range(6):
-        fetch(k).start()
-    fetch(0).wait()
     base = 64 * lax.axis_index("seq") - 32
     for r in range(4):
         for c in range(4):
@@ -424,7 +434,6 @@
     def dot_(a, b):
         return jnp.dot(a, b, preferred_element_type=f32)
 
-    fetch(1).wait()
     for n in range(4):
         w = slice(256 * n, 256 * n + 256)
         s0[:, w] = dot_(nrm[...], wp[:, w]) + pb[:, w]
@@ -439,7 +448,7 @@
             v = v * lax.rsqrt(jnp.mean(v * v, axis=-1, keepdims=True) + EPS) * gl
             lifted[at, :] = v.astype(bf16)
             return 0
-        lax.fori_loop(0, rows // 16, body, 0, unroll=2)
+        lax.fori_loop(0, rows // 16, body, 0, unroll=8)
 
     def module(l, per, lo, keep):
         rows = 4 * per
@@ -476,18 +485,14 @@
         lax.fori_loop(0, 8, depth, 0)
 
     norm(s0, 0, 512)
-    fetch(2).wait()
     module(0, 128, 0, 96)
-    fetch(3).wait()
     for n in range(4):
         w = slice(256 * n, 256 * n + 256)
         d = dot_(act[...], down[0, :, w])
         for r in range(4):
             s1[96 * r:96 * r + 96, w] = s0[128 * r + 16:128 * r + 112, w] + d[96 * r:96 * r + 96]
     norm(s1, 1, 384)
-    fetch(4).wait()
     module(1, 96, 16, 64)
-    fetch(5).wait()
     for n in range(4):
         w = slice(256 * n, 256 * n + 256)
         d = dot_(act[0:256, :], down[1, :, w])
@@ -500,13 +505,9 @@
     return pl.pallas_call(
         conformer_kernel,
         out_shape=jax.ShapeDtypeStruct((4, 64, 1024), bf16),
-        in_specs=[SM, ANY, ANY, VM, VM, ANY, VM, VM, ANY],
+        in_specs=[SM] + [VM] * 8,
         out_specs=VM,
         scratch_shapes=[
-            pltpu.VMEM((8, 64, 512), bf16),
-            pltpu.VMEM((512, 1024), bf16),
-            pltpu.VMEM((2, 1024, 2048), bf16),
-            pltpu.VMEM((2, 1024, 1024), bf16),
             pltpu.VMEM((512, 512), bf16),
             pltpu.VMEM((512, 1024), f32),
             pltpu.VMEM((384, 1024), f32),
@@ -515,9 +516,8 @@
             pltpu.VMEM((512, 256), f32),
             pltpu.VMEM((8, 4, 128, 128), f32),
             pltpu.VMEM((384, 1024), bf16),
-            pltpu.SemaphoreType.DMA((6,)),
         ],
-        compiler_params=pltpu.CompilerParams(vmem_limit_bytes=40 << 20),
+        compiler_params=pltpu.CompilerParams(vmem_limit_bytes=20 << 20),
         name="conform",
     )(lens, recv, wp, pb, gain, up, jnp.transpose(taps, (1, 0, 2)), dbias, down)
 

time: 140 us -> 89.5 us (0.64)
  the two profiles are of different devices: /device:TPU:7 before, /device:TPU:33 now
where the time goes in v2:
time: 89.5 us; the launch traced here: 89.4 us
  Pallas kernels  89.1 us (100%)
    pallas_call x1, Pallas kernels, exchange_frames(): pl.pallas_call(frames_kernel, out_shape=jax.ShapeDtypeStruct((8, 64, 512)...  37.2 us
    pallas_call x1, Pallas kernels, encode(): pl.pallas_call(encoder_kernel, out_shape=jax.ShapeDtypeStruct((320, 512),...  21.6 us
    pallas_call x1, Pallas kernels, conform(): pl.pallas_call(conformer_kernel, out_shape=jax.ShapeDtypeStruct((4, 64, 1...  17.8 us
    pallas_call x1, Pallas kernels, exchange_audio(): pl.pallas_call(audio_kernel, out_shape=(jax.ShapeDtypeStruct((4, 320, 128...  12.4 us

profile of v2, /device:TPU:33, one launch (start us, length us, event | category | flops | bytes accessed | tf_op | source)
XLA Modules:
  0.0 89.4 jit_solution(5720271146813683024)
XLA Ops:
  0.0 0.0 copy-start.7
  0.0 0.0 copy-start.11
  0.0 0.0 copy-start.10
  0.0 0.0 copy-start.4
  0.0 0.0 copy-start.3
  0.0 0.0 copy-start.9
  0.0 0.0 slice-start
  0.1 12.4 %audio.1 = (bf16[4,320,128]{2,1,0:T(8,128)(2,1)S(1)}, bf16[8192,512]{1,0:T(8,128)(2,1)S(1)}, bf16[8,128,512]{2,1,0:T(8,128)(2,1)S(1)}, f32[7,512]{1,0:T(8,128)S(1)}) custom-call(f32[2,40960]{1,0:T(2,128)} %waves_in.1, f32[10,512]{1,0:T(8,128)} %first_in.1, bf16[6144,512]{1,0:T(8,128)(2,1)} %bitcast.12, bf16[2048,512]{1,0:T(8,128)(2,1)} %bitcast.13, ...), custom_call_target="tpu_custom_call" | custom-call | tf_op jit(solution)/shard_map/audio/pallas_call | solution.py:129
  12.5 0.0 copy-start
  12.5 0.0 copy-start.1
  12.5 0.0 copy-start.2
  12.5 0.0 copy-start.5
  12.5 0.0 copy-start.6
  12.6 0.0 copy-start.8
  12.6 0.0 copy-done.7
  12.6 0.0 copy-done.11
  12.6 0.0 copy-done.10
  12.6 0.0 copy-done.4
  12.6 0.0 copy-done.3
  12.6 0.0 copy-done.9
  12.6 0.0 slice-start.1
  12.6 21.6 %encode.1.frames = bf16[320,512]{1,0:T(8,128)(2,1)S(1)} custom-call(s32[4,4]{1,0:T(4,128)S(1)} %copy-done.7, s32[4,4]{1,0:T(4,128)S(1)} %copy-done.9, bf16[4,320,128]{2,1,0:T(8,128)(2,1)S(1)} %get-tuple-element.9.utts_in, bf16[8,128,512]{2,1,0:T(8,128)(2,1)S(1)} %get-tuple-element.10.taps_in, bf16[8192,512]{1,0:T(8,128)(2,1)S(1)} %get-tuple-element.11.w_in, ...), custom_call_target="tpu_custom_call" | custom-call | tf_op jit(solution)/shard_map/encode/pallas_call | solution.py:357
  34.3 37.2 %frames.1.recv = bf16[8,64,512]{2,1,0:T(8,128)(2,1)S(1)} custom-call(bf16[320,512]{1,0:T(8,128)(2,1)S(1)} %encode.1.frames), custom_call_target="tpu_custom_call" | custom-call | tf_op jit(solution)/shard_map/frames/pallas_call | solution.py:415
  71.5 0.0 slice-done
  71.5 0.0 copy-done
  71.5 0.0 copy-done.1
  71.5 0.0 copy-done.2
  71.5 0.0 copy-done.5
  71.5 0.0 copy-done.6
  71.6 0.0 copy-done.8
  71.6 0.0 slice-done.1
  71.6 17.8 %conform.1 = bf16[4,64,1024]{2,1,0:T(8,128)(2,1)} custom-call(s32[4,4]{1,0:T(4,128)S(1)} %copy-done.7, bf16[8,64,512]{2,1,0:T(8,128)(2,1)S(1)} %frames.1.recv, bf16[512,1024]{1,0:T(8,128)(2,1)S(1)} %copy-done.1, f32[1,1024]{1,0:T(1,128)S(1)} %bitcast.9, f32[2,1024]{1,0:T(2,128)S(1)} %copy-done.5, bf16[2,1024,2048]{2,1,0:T(8,128)(2,1)S(1)} %bitcast.7, ...), custom_call_target="tpu_custom_call" | custom-call | tf_op jit(solution)/shard_map/conform/pallas_call | solution.py:505
  (1 shorter events, 0.0 us)
Async XLA Ops:
  0.0 12.6 %copy-start.7 = (s32[4,4]{1,0:T(4,128)S(1)}, s32[4,4]{1,0:T(4,128)}, u32[]{:S(2)}) copy-start(s32[4,4]{1,0:T(4,128)} %lens.3) | copy-start | bytes 196
  0.0 12.6 %copy-start.11 = (f32[512]{0:T(512)S(1)}, f32[512]{0:T(512)}, u32[]{:S(2)}) copy-start(f32[512]{0:T(512)} %param.28) | copy-start | bytes 6148
  0.0 12.6 %copy-start.10 = (f32[512]{0:T(512)S(1)}, f32[512]{0:T(512)}, u32[]{:S(2)}) copy-start(f32[512]{0:T(512)} %param.27) | copy-start | bytes 6148
  0.0 12.6 %copy-start.4 = (f32[7,512]{1,0:T(8,128)S(1)}, f32[7,512]{1,0:T(8,128)}, u32[]{:S(2)}) copy-start(f32[7,512]{1,0:T(8,128)} %shift.1) | copy-start | bytes 43012
  0.0 12.6 %copy-start.3 = (f32[7,512]{1,0:T(8,128)S(1)}, f32[7,512]{1,0:T(8,128)}, u32[]{:S(2)}) copy-start(f32[7,512]{1,0:T(8,128)} %gain.2) | copy-start | bytes 43012
  0.0 12.6 %copy-start.9 = (s32[4,4]{1,0:T(4,128)S(1)}, s32[4,4]{1,0:T(4,128)}, u32[]{:S(2)}) copy-start(s32[4,4]{1,0:T(4,128)} %order.1) | copy-start | bytes 196
  0.0 71.5 %slice-start = ((s8[8388608]{0:T(1024)(128)(4,1)}), s8[4194304]{0:T(1024)(128)(4,1)S(1)}, s32[]{:S(2)}) async-start(s8[8388608]{0:T(1024)(128)(4,1)} %bitcast.6), calls=%async_computation | async-start | bytes 8388608
  12.5 59.0 %copy-start = (bf16[2,1024,1024]{2,1,0:T(8,128)(2,1)S(1)}, bf16[2,1024,1024]{2,1,0:T(8,128)(2,1)}, u32[]{:S(2)}) copy-start(bf16[2,1024,1024]{2,1,0:T(8,128)(2,1)} %down.1) | copy-start | bytes 12582916
  12.5 59.0 %copy-start.1 = (bf16[512,1024]{1,0:T(8,128)(2,1)S(1)}, bf16[512,1024]{1,0:T(8,128)(2,1)}, u32[]{:S(2)}) copy-start(bf16[512,1024]{1,0:T(8,128)(2,1)} %wp.1) | copy-start | bytes 3145732
  12.5 59.0 %copy-start.2 = (f32[2,31,1024]{2,0,1:T(2,128)S(1)}, f32[2,31,1024]{2,0,1:T(2,128)}, u32[]{:S(2)}) copy-start(f32[2,31,1024]{2,0,1:T(2,128)} %param.33) | copy-start | bytes 761860
  12.5 59.0 %copy-start.5 = (f32[2,1024]{1,0:T(2,128)S(1)}, f32[2,1024]{1,0:T(2,128)}, u32[]{:S(2)}) copy-start(f32[2,1024]{1,0:T(2,128)} %gain.3) | copy-start | bytes 24580
  12.5 59.0 %copy-start.6 = (f32[2,1024]{1,0:T(2,128)S(1)}, f32[2,1024]{1,0:T(2,128)}, u32[]{:S(2)}) copy-start(f32[2,1024]{1,0:T(2,128)} %dbias.1) | copy-start | bytes 24580
  12.6 59.0 %copy-start.8 = (f32[1024]{0:T(1024)S(1)}, f32[1024]{0:T(1024)}, u32[]{:S(2)}) copy-start(f32[1024]{0:T(1024)} %param.30) | copy-start | bytes 12292
  12.6 58.9 %slice-start.1 = ((s8[8388608]{0:T(1024)(128)(4,1)}), s8[4194304]{0:T(1024)(128)(4,1)S(1)}, s32[]{:S(2)}) async-start(s8[8388608]{0:T(1024)(128)(4,1)} %bitcast.6), calls=%async_computation.1 | async-start | bytes 8388608

commit v3 on v2

--- a/solution.py
+++ b/solution.py
@@ -15,7 +15,7 @@
 
 
 def audio_kernel(waves_in, first_in, mid, last, bias_in, out, weights, taps, bias,
-                 waves, first, bias_raw, stage, held, raw, w, means, t32, t16, ssem, rsem, wsem, osem):
+                 waves, first, bias_raw, stage, held, raw, w, t32, t16, ssem, rsem, wsem, osem):
     f32, bf16 = jnp.float32, jnp.bfloat16
     dp, seq = lax.axis_index("dp"), lax.axis_index("seq")
     mine = seq == dp // 2
@@ -92,16 +92,12 @@
     ones = jnp.full((512, 128), 1.0 / 512, bf16)
     for b in range(8):
         fetch(b).wait()
-        means[...] = jnp.dot(raw[1024 * b:1024 * b + 1024, :], ones, preferred_element_type=f32)
-
-        def centre(i, _):
-            at = pl.ds(pl.multiple_of(1024 * b + 32 * i, 32), 32)
-            m = means[pl.ds(pl.multiple_of(32 * i, 32), 32), :]
+        for i in range(4):
+            at = slice(1024 * b + 256 * i, 1024 * b + 256 * i + 256)
+            m = jnp.dot(raw[at, :], ones, preferred_element_type=f32)
             for c in range(4):
                 k = slice(128 * c, 128 * c + 128)
                 w[at, k] = (raw[at, k].astype(f32) - m).astype(bf16)
-            return 0
-        lax.fori_loop(0, 32, centre, 0, unroll=4)
         leave(b).start()
 
     for k in range(4):
@@ -140,7 +136,6 @@
             pltpu.VMEM((2, 320, 128), bf16),
             pltpu.VMEM((8192, 512), bf16),
             pltpu.VMEM((8192, 512), bf16),
-            pltpu.VMEM((1024, 128), f32),
             pltpu.VMEM((8, 128, 512), f32),
             pltpu.VMEM((8, 128, 512), bf16),
             pltpu.SemaphoreType.DMA((4,)),
@@ -169,27 +164,14 @@
     return half_gelu((v * r) * gain + shift)
 
 
-def encoder_kernel(lens, order, utts_in, taps_in, w_in, bias, gain, shift, pgain, pshift, out,
-                   utts, taps, w, packed, lhs, y0, y1, e1, e2, e3, e4, e5, e6, halo, out32, sem):
+def encoder_kernel(lens, order, utts, taps, w, bias, gain, shift, pgain, pshift, out,
+                   packed, lhs, y0, y1, e1, e2, e3, e4, e5, e6, halo, out32):
     f32, bf16 = jnp.float32, jnp.bfloat16
     seq = lax.axis_index("seq")
     own, core = seq // 2, seq % 2
-    bounds = (0, 1536, 3072, 4608, 6144, 7168, 8192)
-
-    def fetch(k):
-        if k == 0:
-            return pltpu.make_async_copy(utts_in, utts, sem.at[0])
-        if k == 1:
-            return pltpu.make_async_copy(taps_in, taps, sem.at[1])
-        at = pl.ds(bounds[k - 2], bounds[k - 1] - bounds[k - 2])
-        return pltpu.make_async_copy(w_in.at[at], w.at[at], sem.at[k])
-
-    for k in range(8):
-        fetch(k).start()
     packed[...] = jnp.zeros_like(packed)
     lane = lax.broadcasted_iota(jnp.int32, (320, 128), 1)
     sample = lax.broadcasted_iota(jnp.int32, (320, 128), 0) * 128 + lane
-    fetch(0).wait()
     off = jnp.int32(0)
     for p in range(4):
         u = order[own, p]
@@ -241,7 +223,6 @@
 
     after = packed[pl.ds(80 * core + 80, 8, stride=160), :]
     windows([jnp.concatenate([after, jnp.zeros((8, 128), f32)], axis=0)], 2)
-    fetch(1).wait()
     for v in range(8):
         y0[pl.ds(32 * v, 32), :] = dot_(lhs[0:32, :], taps[v])
 
@@ -249,13 +230,10 @@
         ph = 8 * (k % 2) + k // 2
         e1[pl.ds(16 * (ph // 2), 16), (ph % 2) * 512:(ph % 2) * 512 + 512] = val
     epi(y0, 0, 16, put_first)
-    fetch(2).wait()
     conv3(e1, 0, 0, 112, 16, y0)
     epi(y0, 1, 7, put(e2, 16))
-    fetch(3).wait()
     conv3(e2, 1, 0, 48, 16, y0)
     epi(y0, 2, 3, put(e3, 16))
-    fetch(4).wait()
     conv3(e3, 2, 0, 16, 16, y0)
 
     def keep4(k, val):
@@ -314,8 +292,6 @@
         wrap(e4, 3, i, at, 1024 + at)
         return 0
     lax.fori_loop(0, nv, segment, 0)
-    for k in range(5, 8):
-        fetch(k).wait()
 
     def conv2(src, l, start, y):
         y[...] = dot_(src[pl.ds(start, 256), :], w[6144 + 1024 * l:7168 + 1024 * l, :])
@@ -357,12 +333,9 @@
     return pl.pallas_call(
         encoder_kernel,
         out_shape=jax.ShapeDtypeStruct((320, 512), bf16),
-        in_specs=[SM, SM, HBM, HBM, HBM] + [VM] * 5,
+        in_specs=[SM, SM] + [VM] * 8,
         out_specs=VM,
         scratch_shapes=[
-            pltpu.VMEM((4, 320, 128), bf16),
-            pltpu.VMEM((8, 128, 512), bf16),
-            pltpu.VMEM((8192, 512), bf16),
             pltpu.VMEM((1296, 128), f32),
             pltpu.VMEM((256, 128), bf16),
             pltpu.VMEM((256, 512), f32),
@@ -375,7 +348,6 @@
             pltpu.VMEM((2 * 128, 1024), bf16),
             pltpu.VMEM((64, 512), f32),
             pltpu.VMEM((4, 256, 128), f32),
-            pltpu.SemaphoreType.DMA((8,)),
         ],
         compiler_params=pltpu.CompilerParams(vmem_limit_bytes=30 << 20),
         name="encode",
@@ -434,8 +406,8 @@
     def dot_(a, b):
         return jnp.dot(a, b, preferred_element_type=f32)
 
-    for n in range(4):
-        w = slice(256 * n, 256 * n + 256)
+    halves = (slice(0, 512), slice(512, 1024))
+    for w in halves:
         s0[:, w] = dot_(nrm[...], wp[:, w]) + pb[:, w]
 
     def norm(src, l, rows):
@@ -452,49 +424,51 @@
 
     def module(l, per, lo, keep):
         rows = 4 * per
-
-        def chunk(n, _):
-            wa = pl.ds(pl.multiple_of(256 * n, 256), 256)
-            wb = pl.ds(pl.multiple_of(1024 + 256 * n, 256), 256)
-            ya[0:rows, :] = dot_(lifted[0:rows, :], up[l, :, wa])
-            yb[0:rows, :] = dot_(lifted[0:rows, :], up[l, :, wb])
+        first = 64 - keep // 2
+        ahead = base + lo + lax.broadcasted_iota(jnp.int32, (16, 128), 0)
+
+        def lift(n):
+            ya[0:rows, :] = dot_(lifted[0:rows, :], up[l, :, 512 * n:512 * n + 512])
+            yb[0:rows, :] = dot_(lifted[0:rows, :], up[l, :, 1024 + 512 * n:1536 + 512 * n])
+
+        def gate(n):
             for r in range(4):
                 total = lens[r, 0] + lens[r, 1] + lens[r, 2] + lens[r, 3]
                 valid = (total - 400) // 320 + 1
                 for k in range(per // 16):
                     at = slice(per * r + 16 * k, per * r + 16 * k + 16)
-                    t = base + lo + 16 * k + lax.broadcasted_iota(jnp.int32, (16, 256), 0)
+                    t = ahead + 16 * k
                     live = jnp.logical_and(t >= 0, t < valid)
-                    v = jnp.where(live, ya[at, :] * jax.nn.sigmoid(yb[at, :]), 0.0)
-                    g[2 * n, r, lo + 16 * k:lo + 16 * k + 16, :] = v[:, 0:128]
-                    g[2 * n + 1, r, lo + 16 * k:lo + 16 * k + 16, :] = v[:, 128:256]
+                    for c in range(4):
+                        w = slice(128 * c, 128 * c + 128)
+                        v = ya[at, w] * jax.nn.sigmoid(yb[at, w])
+                        g[4 * n + c, r, lo + 16 * k:lo + 16 * k + 16, :] = jnp.where(live, v, 0.0)
+
+        def block(c, r, w):
+            acc = jnp.broadcast_to(dbias[l:l + 1, w], (keep, 128))
+            for j in range(31):
+                acc = acc + g[c, r, first + j - 15:first + j - 15 + keep, :] * taps[j, l:l + 1, w]
+            act[keep * r:keep * r + keep, w] = (acc * jax.nn.sigmoid(acc)).astype(bf16)
+
+        def depth(c, _):
+            for r in range(4):
+                block(c, r, pl.ds(pl.multiple_of(128 * c, 128), 128))
             return 0
-        lax.fori_loop(0, 4, chunk, 0)
-        first = 64 - keep // 2
-
-        def depth(c, _):
-            w = pl.ds(pl.multiple_of(128 * c, 128), 128)
-
-            def one(r, _):
-                acc = jnp.broadcast_to(dbias[l:l + 1, w], (keep, 128))
-                for j in range(31):
-                    acc = acc + g[c, r, first + j - 15:first + j - 15 + keep, :] * taps[j, l:l + 1, w]
-                act[pl.ds(pl.multiple_of(keep * r, 32), keep), w] = (acc * jax.nn.sigmoid(acc)).astype(bf16)
-                return 0
-            return lax.fori_loop(0, 4, one, 0)
+        lift(0)
+        gate(0)
+        lift(1)
+        gate(1)
         lax.fori_loop(0, 8, depth, 0)
 
     norm(s0, 0, 512)
     module(0, 128, 0, 96)
-    for n in range(4):
-        w = slice(256 * n, 256 * n + 256)
+    for w in halves:
         d = dot_(act[...], down[0, :, w])
         for r in range(4):
             s1[96 * r:96 * r + 96, w] = s0[128 * r + 16:128 * r + 112, w] + d[96 * r:96 * r + 96]
     norm(s1, 1, 384)
     module(1, 96, 16, 64)
-    for n in range(4):
-        w = slice(256 * n, 256 * n + 256)
+    for w in halves:
         d = dot_(act[0:256, :], down[1, :, w])
         for r in range(4):
             out[r, :, w] = (s1[96 * r + 16:96 * r + 80, w] + d[64 * r:64 * r + 64]).astype(bf16)
@@ -512,8 +486,8 @@
             pltpu.VMEM((512, 1024), f32),
             pltpu.VMEM((384, 1024), f32),
             pltpu.VMEM((512, 1024), bf16),
-            pltpu.VMEM((512, 256), f32),
-            pltpu.VMEM((512, 256), f32),
+            pltpu.VMEM((512, 512), f32),
+            pltpu.VMEM((512, 512), f32),
             pltpu.VMEM((8, 4, 128, 128), f32),
             pltpu.VMEM((384, 1024), bf16),
         ],

time: 89.5 us -> 87.1 us (0.973)
  the two profiles are of different devices: /device:TPU:33 before, /device:TPU:37 now
where the time goes in v3:
time: 87.1 us; the launch traced here: 87 us
  Pallas kernels  86.7 us (100%)
    pallas_call x1, Pallas kernels, encode(): pl.pallas_call(encoder_kernel, out_shape=jax.ShapeDtypeStruct((320, 512),...  29.9 us
    pallas_call x1, Pallas kernels, exchange_audio(): pl.pallas_call(audio_kernel, out_shape=(jax.ShapeDtypeStruct((4, 320, 128...  22.6 us
    pallas_call x1, Pallas kernels, exchange_frames(): pl.pallas_call(frames_kernel, out_shape=jax.ShapeDtypeStruct((8, 64, 512)...  18.4 us
    pallas_call x1, Pallas kernels, conform(): pl.pallas_call(conformer_kernel, out_shape=jax.ShapeDtypeStruct((4, 64, 1...  15.8 us

profile of v3, /device:TPU:37, one launch (start us, length us, event | category | flops | bytes accessed | tf_op | source)
XLA Modules:
  0.0 87.0 jit_solution(14987217304840656480)
XLA Ops:
  0.0 0.0 copy-start.7
  0.0 0.0 copy-start.11
  0.0 0.0 copy-start.10
  0.0 0.0 copy-start.4
  0.0 0.0 copy-start.3
  0.0 0.0 copy-start.9
  0.0 0.0 slice-start
  0.1 22.6 %audio.1 = (bf16[4,320,128]{2,1,0:T(8,128)(2,1)S(1)}, bf16[8192,512]{1,0:T(8,128)(2,1)S(1)}, bf16[8,128,512]{2,1,0:T(8,128)(2,1)S(1)}, f32[7,512]{1,0:T(8,128)S(1)}) custom-call(f32[2,40960]{1,0:T(2,128)} %waves_in.1, f32[10,512]{1,0:T(8,128)} %first_in.1, bf16[6144,512]{1,0:T(8,128)(2,1)} %bitcast.12, bf16[2048,512]{1,0:T(8,128)(2,1)} %bitcast.13, ...), custom_call_target="tpu_custom_call" | custom-call | tf_op jit(solution)/shard_map/audio/pallas_call | solution.py:125
  22.7 0.0 copy-start
  22.7 0.0 copy-start.1
  22.7 0.0 copy-start.2
  22.7 0.0 copy-start.5
  22.7 0.0 copy-start.6
  22.7 0.0 copy-start.8
  22.7 0.0 copy-done.7
  22.8 0.0 copy-done.11
  22.8 0.0 copy-done.10
  22.8 0.0 copy-done.4
  22.8 0.0 copy-done.3
  22.8 0.0 copy-done.9
  22.8 0.0 slice-start.1
  22.8 29.9 %encode.1.frames = bf16[320,512]{1,0:T(8,128)(2,1)S(1)} custom-call(s32[4,4]{1,0:T(4,128)S(1)} %copy-done.7, s32[4,4]{1,0:T(4,128)S(1)} %copy-done.9, bf16[4,320,128]{2,1,0:T(8,128)(2,1)S(1)} %get-tuple-element.9.utts, bf16[8,128,512]{2,1,0:T(8,128)(2,1)S(1)} %get-tuple-element.10.taps, bf16[8192,512]{1,0:T(8,128)(2,1)S(1)} %get-tuple-element.11.w, ...), custom_call_target="tpu_custom_call" | custom-call | tf_op jit(solution)/shard_map/encode/pallas_call | solution.py:333
  52.7 18.4 %frames.1.recv = bf16[8,64,512]{2,1,0:T(8,128)(2,1)S(1)} custom-call(bf16[320,512]{1,0:T(8,128)(2,1)S(1)} %encode.1.frames), custom_call_target="tpu_custom_call" | custom-call | tf_op jit(solution)/shard_map/frames/pallas_call | solution.py:387
  71.2 0.0 slice-done
  71.2 0.0 copy-done
  71.2 0.0 copy-done.1
  71.2 0.0 copy-done.2
  71.2 0.0 copy-done.5
  71.2 0.0 copy-done.6
  71.2 0.0 copy-done.8
  71.2 0.0 slice-done.1
  71.3 15.8 %conform.1 = bf16[4,64,1024]{2,1,0:T(8,128)(2,1)} custom-call(s32[4,4]{1,0:T(4,128)S(1)} %copy-done.7, bf16[8,64,512]{2,1,0:T(8,128)(2,1)S(1)} %frames.1.recv, bf16[512,1024]{1,0:T(8,128)(2,1)S(1)} %copy-done.1, f32[1,1024]{1,0:T(1,128)S(1)} %bitcast.9, f32[2,1024]{1,0:T(2,128)S(1)} %copy-done.5, bf16[2,1024,2048]{2,1,0:T(8,128)(2,1)S(1)} %bitcast.7, ...), custom_call_target="tpu_custom_call" | custom-call | tf_op jit(solution)/shard_map/conform/pallas_call | solution.py:479
  (1 shorter events, 0.0 us)
Async XLA Ops:
  0.0 22.7 %copy-start.7 = (s32[4,4]{1,0:T(4,128)S(1)}, s32[4,4]{1,0:T(4,128)}, u32[]{:S(2)}) copy-start(s32[4,4]{1,0:T(4,128)} %lens.3) | copy-start | bytes 196
  0.0 22.8 %copy-start.11 = (f32[512]{0:T(512)S(1)}, f32[512]{0:T(512)}, u32[]{:S(2)}) copy-start(f32[512]{0:T(512)} %param.28) | copy-start | bytes 6148
  0.0 22.8 %copy-start.10 = (f32[512]{0:T(512)S(1)}, f32[512]{0:T(512)}, u32[]{:S(2)}) copy-start(f32[512]{0:T(512)} %param.27) | copy-start | bytes 6148
  0.0 22.8 %copy-start.4 = (f32[7,512]{1,0:T(8,128)S(1)}, f32[7,512]{1,0:T(8,128)}, u32[]{:S(2)}) copy-start(f32[7,512]{1,0:T(8,128)} %shift.1) | copy-start | bytes 43012
  0.0 22.8 %copy-start.3 = (f32[7,512]{1,0:T(8,128)S(1)}, f32[7,512]{1,0:T(8,128)}, u32[]{:S(2)}) copy-start(f32[7,512]{1,0:T(8,128)} %gain.2) | copy-start | bytes 43012
  0.0 22.8 %copy-start.9 = (s32[4,4]{1,0:T(4,128)S(1)}, s32[4,4]{1,0:T(4,128)}, u32[]{:S(2)}) copy-start(s32[4,4]{1,0:T(4,128)} %order.1) | copy-start | bytes 196
  0.0 71.1 %slice-start = ((s8[8388608]{0:T(1024)(128)(4,1)}), s8[4194304]{0:T(1024)(128)(4,1)S(1)}, s32[]{:S(2)}) async-start(s8[8388608]{0:T(1024)(128)(4,1)} %bitcast.6), calls=%async_computation | async-start | bytes 8388608
  22.7 48.5 %copy-start = (bf16[2,1024,1024]{2,1,0:T(8,128)(2,1)S(1)}, bf16[2,1024,1024]{2,1,0:T(8,128)(2,1)}, u32[]{:S(2)}) copy-start(bf16[2,1024,1024]{2,1,0:T(8,128)(2,1)} %down.1) | copy-start | bytes 12582916
  22.7 48.5 %copy-start.1 = (bf16[512,1024]{1,0:T(8,128)(2,1)S(1)}, bf16[512,1024]{1,0:T(8,128)(2,1)}, u32[]{:S(2)}) copy-start(bf16[512,1024]{1,0:T(8,128)(2,1)} %wp.1) | copy-start | bytes 3145732
  22.7 48.5 %copy-start.2 = (f32[2,31,1024]{2,0,1:T(2,128)S(1)}, f32[2,31,1024]{2,0,1:T(2,128)}, u32[]{:S(2)}) copy-start(f32[2,31,1024]{2,0,1:T(2,128)} %param.33) | copy-start | bytes 761860
  22.7 48.5 %copy-start.5 = (f32[2,1024]{1,0:T(2,128)S(1)}, f32[2,1024]{1,0:T(2,128)}, u32[]{:S(2)}) copy-start(f32[2,1024]{1,0:T(2,128)} %gain.3) | copy-start | bytes 24580
  22.7 48.5 %copy-start.6 = (f32[2,1024]{1,0:T(2,128)S(1)}, f32[2,1024]{1,0:T(2,128)}, u32[]{:S(2)}) copy-start(f32[2,1024]{1,0:T(2,128)} %dbias.1) | copy-start | bytes 24580
  22.7 48.5 %copy-start.8 = (f32[1024]{0:T(1024)S(1)}, f32[1024]{0:T(1024)}, u32[]{:S(2)}) copy-start(f32[1024]{0:T(1024)} %param.30) | copy-start | bytes 12292
  22.8 48.4 %slice-start.1 = ((s8[8388608]{0:T(1024)(128)(4,1)}), s8[4194304]{0:T(1024)(128)(4,1)S(1)}, s32[]{:S(2)}) async-start(s8[8388608]{0:T(1024)(128)(4,1)} %bitcast.6), calls=%async_computation.1 | async-start | bytes 8388608

commit v4 on v3

--- a/solution.py
+++ b/solution.py
@@ -83,7 +83,7 @@
     fw = first[...] - jnp.mean(first[...], axis=-1, keepdims=True)
     hi = b0[0:1].astype(bf16).astype(f32)
     t32[...] = jnp.zeros_like(t32)
-    for v in range(8):
+    for v in range(4):
         t32[v, 5 * v:5 * v + 10, :] = fw
         t32[v, 126:127, :] = hi
         t32[v, 127:128, :] = b0[0:1] - hi
@@ -125,7 +125,7 @@
     return pl.pallas_call(
         audio_kernel,
         out_shape=(jax.ShapeDtypeStruct((4, 320, 128), bf16), jax.ShapeDtypeStruct((8192, 512), bf16),
-                   jax.ShapeDtypeStruct((8, 128, 512), bf16), jax.ShapeDtypeStruct((7, 512), f32)),
+                   jax.ShapeDtypeStruct((4, 128, 512), bf16), jax.ShapeDtypeStruct((7, 512), f32)),
         in_specs=[HBM, HBM, HBM, HBM, HBM],
         out_specs=(HBM, HBM, HBM, VM),
         scratch_shapes=[
@@ -136,8 +136,8 @@
             pltpu.VMEM((2, 320, 128), bf16),
             pltpu.VMEM((8192, 512), bf16),
             pltpu.VMEM((8192, 512), bf16),
-            pltpu.VMEM((8, 128, 512), f32),
-            pltpu.VMEM((8, 128, 512), bf16),
+            pltpu.VMEM((4, 128, 512), f32),
+            pltpu.VMEM((4, 128, 512), bf16),
             pltpu.SemaphoreType.DMA((4,)),
             pltpu.SemaphoreType.DMA((4,)),
             pltpu.SemaphoreType.DMA((11,)),
@@ -162,6 +162,10 @@
     ss = jnp.sum(v * v, axis=-1, keepdims=True)
     r = lax.rsqrt(ss * (1.0 / 512) + EPS)
     return half_gelu((v * r) * gain + shift)
+
+
+class Held:
+    v = None
 
 
 def encoder_kernel(lens, order, utts, taps, w, bias, gain, shift, pgain, pshift, out,
@@ -190,19 +194,28 @@
     def dot_(a, b):
         return jnp.dot(a, b, preferred_element_type=f32)
 
-    def epi(y, l, groups, dst):
+    def epi(y, l, groups, dst, nxt=None):
         g, s = row(gain, l) * 0.5, row(shift, l) * 0.5
         b = row(bias, l)
         for k in range(groups):
-            v = y[pl.ds(16 * k, 16), :]
+            if k % 8 == 0 and isinstance(y, Held):
+                if len(y.v) <= k // 8:
+                    y.v.append(y.jobs.pop(0)())
+                if nxt is not None and nxt.jobs:
+                    nxt.v.append(nxt.jobs.pop(0)())
+            v = y.v[k // 8][16 * (k % 8):16 * (k % 8) + 16] if isinstance(y, Held) else y[pl.ds(16 * k, 16), :]
             if l > 0:
                 v = v + b
             dst(k, finish(v, g, s))
 
     def conv3(src, l, start, rows, gap, y):
         at = 1536 * l
-        y[pl.ds(0, rows), :] = dot_(src[pl.ds(start, rows), :], w[at:at + 1024, :]) + dot_(
-            src[pl.ds(start + gap, rows), 0:512], w[at + 1024:at + 1536, :])
+        if not isinstance(y, Held):
+            y[pl.ds(0, rows), :] = dot_(src[pl.ds(start, rows), :], w[at:at + 1024, :]) + dot_(
+                src[pl.ds(start + gap, rows), 0:512], w[at + 1024:at + 1536, :])
+            return
+        y.v, y.jobs = [], [lambda o=o: dot_(src[pl.ds(start + o, 128), :], w[at:at + 1024, :]) + dot_(
+            src[pl.ds(start + gap + o, 128), 0:512], w[at + 1024:at + 1536, :]) for o in range(0, rows, 128)]
 
     def put(ref, gap, base=0):
         def at(k, v):
@@ -214,20 +227,20 @@
 
     def windows(cols, count):
         for q in range(count):
-            j, o = divmod(40 * q, 128)
+            j, o = divmod(20 * q, 128)
             x = cols[j] if o == 0 else pltpu.roll(cols[j], 128 - o, 1)
-            if o + 45 > 128:
+            if o + 25 > 128:
                 x = jnp.where(lane16 < 128 - o, x, pltpu.roll(cols[j + 1], 128 - o, 1))
             x = jnp.where(lane16 >= 126, 1.0, x)
             lhs[pl.ds(16 * q, 16), :] = x.astype(bf16)
 
     after = packed[pl.ds(80 * core + 80, 8, stride=160), :]
-    windows([jnp.concatenate([after, jnp.zeros((8, 128), f32)], axis=0)], 2)
-    for v in range(8):
-        y0[pl.ds(32 * v, 32), :] = dot_(lhs[0:32, :], taps[v])
+    windows([jnp.concatenate([after, jnp.zeros((8, 128), f32)], axis=0)], 4)
+    for v in range(4):
+        y0[pl.ds(64 * v, 64), :] = dot_(lhs[0:64, :], taps[v])
 
     def put_first(k, val):
-        ph = 8 * (k % 2) + k // 2
+        ph = 4 * (k % 4) + k // 4
         e1[pl.ds(16 * (ph // 2), 16), (ph % 2) * 512:(ph % 2) * 512 + 512] = val
     epi(y0, 0, 16, put_first)
     conv3(e1, 0, 0, 112, 16, y0)
@@ -256,34 +269,35 @@
 
     def segment(i, _):
         base = 5 * (32 * i + 16 * core)
-        windows([packed[pl.ds(base + j, 16, stride=5), :] for j in range(6)], 16)
+        windows([packed[pl.ds(base + j, 16, stride=5), :] for j in range(6)], 32)
+        y0, y1 = Held(), Held()
 
         def first(v, y):
-            y[...] = dot_(lhs[...], taps[v])
+            y.v, y.jobs = [], [lambda o=o: dot_(lhs[o:o + 128, :], taps[v]) for o in range(0, 512, 128)]
 
         def put1(v):
             def at(q, val):
-                e1[pl.ds(64 * q + 16 * (v // 2), 16), 512 * (v % 2):512 * (v % 2) + 512] = val
+                e1[pl.ds(32 * q + 16 * (v // 2), 16), 512 * (v % 2):512 * (v % 2) + 512] = val
             return at
         ys = (y0, y1)
         first(0, y0)
-        for v in range(8):
-            if v < 7:
+        for v in range(4):
+            if v < 3:
                 first(v + 1, ys[(v + 1) % 2])
-            epi(ys[v % 2], 0, 16, put1(v))
+            epi(ys[v % 2], 0, 32, put1(v), ys[(v + 1) % 2] if v < 3 else None)
         wrap(e1, 0, i, 0, 1024)
         conv3(e1, 0, 0, 256, 16, y0)
         conv3(e1, 0, 256, 256, 16, y1)
-        epi(y0, 1, 16, put(e2, 16, 0))
+        epi(y0, 1, 16, put(e2, 16, 0), y1)
         conv3(e1, 0, 512, 256, 16, y0)
-        epi(y1, 1, 16, put(e2, 16, 128))
+        epi(y1, 1, 16, put(e2, 16, 128), y0)
         conv3(e1, 0, 768, 256, 16, y1)
-        epi(y0, 1, 16, put(e2, 16, 256))
+        epi(y0, 1, 16, put(e2, 16, 256), y1)
         conv3(e2, 1, 0, 256, 16, y0)
-        epi(y1, 1, 16, put(e2, 16, 384))
+        epi(y1, 1, 16, put(e2, 16, 384), y0)
         wrap(e2, 1, i, 0, 512)
         conv3(e2, 1, 256, 256, 16, y1)
-        epi(y0, 2, 16, put(e3, 16, 0))
+        epi(y0, 2, 16, put(e3, 16, 0), y1)
         epi(y1, 2, 16, put(e3, 16, 128))
         wrap(e3, 2, i, 0, 256)
         conv3(e3, 2, 0, 256, 16, y0)
@@ -294,23 +308,24 @@
     lax.fori_loop(0, nv, segment, 0)
 
     def conv2(src, l, start, y):
-        y[...] = dot_(src[pl.ds(start, 256), :], w[6144 + 1024 * l:7168 + 1024 * l, :])
+        y.v, y.jobs = [], [lambda o=o: dot_(src[pl.ds(start + o, 128), :], w[6144 + 1024 * l:7168 + 1024 * l, :]) for o in (0, 128)]
 
     def put8(ref, base):
         def at(k, v):
             ref[pl.ds(base + 16 * (k % 8), 16), (k // 8) * 512:(k // 8) * 512 + 512] = v
         return at
+    y0, y1 = Held(), Held()
     conv3(e4, 3, 0, 256, 128, y0)
     conv3(e4, 3, 256, 256, 128, y1)
-    epi(y0, 4, 16, put8(e5, 0))
+    epi(y0, 4, 16, put8(e5, 0), y1)
     conv3(e4, 3, 512, 256, 128, y0)
-    epi(y1, 4, 16, put8(e5, 128))
+    epi(y1, 4, 16, put8(e5, 128), y0)
     conv3(e4, 3, 768, 256, 128, y1)
-    epi(y0, 4, 16, put8(e5, 256))
+    epi(y0, 4, 16, put8(e5, 256), y1)
     conv2(e5, 0, 0, y0)
-    epi(y1, 4, 16, put8(e5, 384))
+    epi(y1, 4, 16, put8(e5, 384), y0)
     conv2(e5, 0, 256, y1)
-    epi(y0, 5, 16, put8(e6, 0))
+    epi(y0, 5, 16, put8(e6, 0), y1)
     epi(y1, 5, 16, put8(e6, 128))
     conv2(e6, 1, 0, y0)
     pg, ps = pgain[...], pshift[...]
@@ -337,9 +352,9 @@
         out_specs=VM,
         scratch_shapes=[
             pltpu.VMEM((1296, 128), f32),
-            pltpu.VMEM((256, 128), bf16),
-            pltpu.VMEM((256, 512), f32),
-            pltpu.VMEM((256, 512), f32),
+            pltpu.VMEM((512, 128), bf16),
+            pltpu.VMEM((512, 512), f32),
+            pltpu.VMEM((512, 512), f32),
             pltpu.VMEM((65 * 16, 1024), bf16),
             pltpu.VMEM((33 * 16, 1024), bf16),
             pltpu.VMEM((17 * 16, 1024), bf16),
@@ -420,7 +435,7 @@
             v = v * lax.rsqrt(jnp.mean(v * v, axis=-1, keepdims=True) + EPS) * gl
             lifted[at, :] = v.astype(bf16)
             return 0
-        lax.fori_loop(0, rows // 16, body, 0, unroll=8)
+        lax.fori_loop(0, rows // 16, body, 0, unroll=True)
 
     def module(l, per, lo, keep):
         rows = 4 * per

time: 87.1 us -> 83.2 us (0.955)
  the two profiles are of different devices: /device:TPU:37 before, /device:TPU:71 now
where the time goes in v4:
time: 83.2 us; the launch traced here: 83.1 us
  Pallas kernels  82.8 us (100%)
    pallas_call x1, Pallas kernels, encode(): pl.pallas_call(encoder_kernel, out_shape=jax.ShapeDtypeStruct((320, 512),...  38.7 us
    pallas_call x1, Pallas kernels, exchange_audio(): pl.pallas_call(audio_kernel, out_shape=(jax.ShapeDtypeStruct((4, 320, 128...  19.7 us
    pallas_call x1, Pallas kernels, conform(): pl.pallas_call(conformer_kernel, out_shape=jax.ShapeDtypeStruct((4, 64, 1...  14.6 us
    pallas_call x1, Pallas kernels, exchange_frames(): pl.pallas_call(frames_kernel, out_shape=jax.ShapeDtypeStruct((8, 64, 512)...  9.84 us

profile of v4, /device:TPU:71, one launch (start us, length us, event | category | flops | bytes accessed | tf_op | source)
XLA Modules:
  0.0 83.1 jit_solution(16674354770019459828)
XLA Ops:
  0.0 0.0 copy-start.7
  0.0 0.0 copy-start.11
  0.0 0.0 copy-start.10
  0.0 0.0 copy-start.4
  0.0 0.0 copy-start.3
  0.0 0.0 copy-start.9
  0.0 0.0 slice-start
  0.1 19.7 %audio.1 = (bf16[4,320,128]{2,1,0:T(8,128)(2,1)S(1)}, bf16[8192,512]{1,0:T(8,128)(2,1)S(1)}, bf16[4,128,512]{2,1,0:T(8,128)(2,1)S(1)}, f32[7,512]{1,0:T(8,128)S(1)}) custom-call(f32[2,40960]{1,0:T(2,128)} %waves_in.1, f32[10,512]{1,0:T(8,128)} %first_in.1, bf16[6144,512]{1,0:T(8,128)(2,1)} %bitcast.12, bf16[2048,512]{1,0:T(8,128)(2,1)} %bitcast.13, ...), custom_call_target="tpu_custom_call" | custom-call | tf_op jit(solution)/shard_map/audio/pallas_call | solution.py:125
  19.8 0.0 copy-start
  19.8 0.0 copy-start.1
  19.8 0.0 copy-start.2
  19.8 0.0 copy-start.5
  19.8 0.0 copy-start.6
  19.8 0.0 copy-start.8
  19.8 0.0 copy-done.7
  19.8 0.0 copy-done.11
  19.8 0.0 copy-done.10
  19.9 0.0 copy-done.4
  19.9 0.0 copy-done.3
  19.9 0.0 copy-done.9
  19.9 0.0 slice-start.1
  19.9 38.7 %encode.1.frames = bf16[320,512]{1,0:T(8,128)(2,1)S(1)} custom-call(s32[4,4]{1,0:T(4,128)S(1)} %copy-done.7, s32[4,4]{1,0:T(4,128)S(1)} %copy-done.9, bf16[4,320,128]{2,1,0:T(8,128)(2,1)S(1)} %get-tuple-element.9.utts, bf16[4,128,512]{2,1,0:T(8,128)(2,1)S(1)} %get-tuple-element.10.taps, bf16[8192,512]{1,0:T(8,128)(2,1)S(1)} %get-tuple-element.11.w, ...), custom_call_target="tpu_custom_call" | custom-call | tf_op jit(solution)/shard_map/encode/pallas_call | solution.py:348
  58.6 9.8 %frames.1.recv = bf16[8,64,512]{2,1,0:T(8,128)(2,1)S(1)} custom-call(bf16[320,512]{1,0:T(8,128)(2,1)S(1)} %encode.1.frames), custom_call_target="tpu_custom_call" | custom-call | tf_op jit(solution)/shard_map/frames/pallas_call | solution.py:402
  68.5 0.0 slice-done
  68.5 0.0 copy-done
  68.5 0.0 copy-done.1
  68.5 0.0 copy-done.2
  68.5 0.0 copy-done.5
  68.5 0.0 copy-done.6
  68.5 0.0 copy-done.8
  68.6 0.0 slice-done.1
  68.6 14.6 %conform.1 = bf16[4,64,1024]{2,1,0:T(8,128)(2,1)} custom-call(s32[4,4]{1,0:T(4,128)S(1)} %copy-done.7, bf16[8,64,512]{2,1,0:T(8,128)(2,1)S(1)} %frames.1.recv, bf16[512,1024]{1,0:T(8,128)(2,1)S(1)} %copy-done.1, f32[1,1024]{1,0:T(1,128)S(1)} %bitcast.9, f32[2,1024]{1,0:T(2,128)S(1)} %copy-done.5, bf16[2,1024,2048]{2,1,0:T(8,128)(2,1)S(1)} %bitcast.7, ...), custom_call_target="tpu_custom_call" | custom-call | tf_op jit(solution)/shard_map/conform/pallas_call | solution.py:494
  (1 shorter events, 0.0 us)
Async XLA Ops:
  0.0 19.8 %copy-start.7 = (s32[4,4]{1,0:T(4,128)S(1)}, s32[4,4]{1,0:T(4,128)}, u32[]{:S(2)}) copy-start(s32[4,4]{1,0:T(4,128)} %lens.3) | copy-start | bytes 196
  0.0 19.8 %copy-start.11 = (f32[512]{0:T(512)S(1)}, f32[512]{0:T(512)}, u32[]{:S(2)}) copy-start(f32[512]{0:T(512)} %param.28) | copy-start | bytes 6148
  0.0 19.8 %copy-start.10 = (f32[512]{0:T(512)S(1)}, f32[512]{0:T(512)}, u32[]{:S(2)}) copy-start(f32[512]{0:T(512)} %param.27) | copy-start | bytes 6148
  0.0 19.8 %copy-start.4 = (f32[7,512]{1,0:T(8,128)S(1)}, f32[7,512]{1,0:T(8,128)}, u32[]{:S(2)}) copy-start(f32[7,512]{1,0:T(8,128)} %shift.1) | copy-start | bytes 43012
  0.0 19.8 %copy-start.3 = (f32[7,512]{1,0:T(8,128)S(1)}, f32[7,512]{1,0:T(8,128)}, u32[]{:S(2)}) copy-start(f32[7,512]{1,0:T(8,128)} %gain.2) | copy-start | bytes 43012
  0.0 19.8 %copy-start.9 = (s32[4,4]{1,0:T(4,128)S(1)}, s32[4,4]{1,0:T(4,128)}, u32[]{:S(2)}) copy-start(s32[4,4]{1,0:T(4,128)} %order.1) | copy-start | bytes 196
  0.0 68.5 %slice-start = ((s8[8388608]{0:T(1024)(128)(4,1)}), s8[4194304]{0:T(1024)(128)(4,1)S(1)}, s32[]{:S(2)}) async-start(s8[8388608]{0:T(1024)(128)(4,1)} %bitcast.6), calls=%async_computation | async-start | bytes 8388608
  19.8 48.7 %copy-start = (bf16[2,1024,1024]{2,1,0:T(8,128)(2,1)S(1)}, bf16[2,1024,1024]{2,1,0:T(8,128)(2,1)}, u32[]{:S(2)}) copy-start(bf16[2,1024,1024]{2,1,0:T(8,128)(2,1)} %down.1) | copy-start | bytes 12582916
  19.8 48.7 %copy-start.1 = (bf16[512,1024]{1,0:T(8,128)(2,1)S(1)}, bf16[512,1024]{1,0:T(8,128)(2,1)}, u32[]{:S(2)}) copy-start(bf16[512,1024]{1,0:T(8,128)(2,1)} %wp.1) | copy-start | bytes 3145732
  19.8 48.7 %copy-start.2 = (f32[2,31,1024]{2,0,1:T(2,128)S(1)}, f32[2,31,1024]{2,0,1:T(2,128)}, u32[]{:S(2)}) copy-start(f32[2,31,1024]{2,0,1:T(2,128)} %param.33) | copy-start | bytes 761860
  19.8 48.7 %copy-start.5 = (f32[2,1024]{1,0:T(2,128)S(1)}, f32[2,1024]{1,0:T(2,128)}, u32[]{:S(2)}) copy-start(f32[2,1024]{1,0:T(2,128)} %gain.3) | copy-start | bytes 24580
  19.8 48.7 %copy-start.6 = (f32[2,1024]{1,0:T(2,128)S(1)}, f32[2,1024]{1,0:T(2,128)}, u32[]{:S(2)}) copy-start(f32[2,1024]{1,0:T(2,128)} %dbias.1) | copy-start | bytes 24580
  19.8 48.7 %copy-start.8 = (f32[1024]{0:T(1024)S(1)}, f32[1024]{0:T(1024)}, u32[]{:S(2)}) copy-start(f32[1024]{0:T(1024)} %param.30) | copy-start | bytes 12292
  19.9 48.7 %slice-start.1 = ((s8[8388608]{0:T(1024)(128)(4,1)}), s8[4194304]{0:T(1024)(128)(4,1)S(1)}, s32[]{:S(2)}) async-start(s8[8388608]{0:T(1024)(128)(4,1)} %bitcast.6), calls=%async_computation.1 | async-start | bytes 8388608

commit v5 on v4

--- a/solution.py
+++ b/solution.py
@@ -15,7 +15,7 @@
 
 
 def audio_kernel(waves_in, first_in, mid, last, bias_in, out, weights, taps, bias,
-                 waves, first, bias_raw, stage, held, raw, w, t32, t16, ssem, rsem, wsem, osem):
+                 waves, first, bias_raw, stage, held, raw, t32, ssem, rsem, wsem):
     f32, bf16 = jnp.float32, jnp.bfloat16
     dp, seq = lax.axis_index("dp"), lax.axis_index("seq")
     mine = seq == dp // 2
@@ -32,10 +32,6 @@
     def fetch(b):
         src = mid.at[pl.ds(1024 * b, 1024)] if b < 6 else last.at[pl.ds(1024 * (b - 6), 1024)]
         return pltpu.make_async_copy(src, raw.at[pl.ds(1024 * b, 1024)], wsem.at[b])
-
-    def leave(b):
-        at = pl.ds(1024 * b, 1024)
-        return pltpu.make_async_copy(w.at[at], weights.at[at], osem.at[b])
 
     small = [pltpu.make_async_copy(x, y, wsem.at[8 + k]) for k, (x, y) in enumerate(
         ((waves_in, waves), (first_in, first), (bias_in, bias_raw)))]
@@ -87,8 +83,7 @@
         t32[v, 5 * v:5 * v + 10, :] = fw
         t32[v, 126:127, :] = hi
         t32[v, 127:128, :] = b0[0:1] - hi
-    t16[...] = t32[...].astype(bf16)
-    pltpu.make_async_copy(t16, taps, osem.at[8]).start()
+    taps[...] = t32[...].astype(bf16)
     ones = jnp.full((512, 128), 1.0 / 512, bf16)
     for b in range(8):
         fetch(b).wait()
@@ -97,8 +92,7 @@
             m = jnp.dot(raw[at, :], ones, preferred_element_type=f32)
             for c in range(4):
                 k = slice(128 * c, 128 * c + 128)
-                w[at, k] = (raw[at, k].astype(f32) - m).astype(bf16)
-        leave(b).start()
+                weights[at, k] = (raw[at, k].astype(f32) - m).astype(bf16)
 
     for k in range(4):
         @pl.when(jnp.logical_not(jnp.logical_and(mine, slot == k)))
@@ -115,9 +109,6 @@
             @pl.when(here(e, c))
             def _():
                 local(e, c).wait()
-    pltpu.make_async_copy(t16, taps, osem.at[8]).wait()
-    for b in range(8):
-        leave(b).wait()
 
 
 def exchange_audio(waves, first, mid, last, bias):
@@ -127,7 +118,7 @@
         out_shape=(jax.ShapeDtypeStruct((4, 320, 128), bf16), jax.ShapeDtypeStruct((8192, 512), bf16),
                    jax.ShapeDtypeStruct((4, 128, 512), bf16), jax.ShapeDtypeStruct((7, 512), f32)),
         in_specs=[HBM, HBM, HBM, HBM, HBM],
-        out_specs=(HBM, HBM, HBM, VM),
+        out_specs=(HBM, VM, VM, VM),
         scratch_shapes=[
             pltpu.VMEM((2, 40960), f32),
             pltpu.VMEM((10, 512), f32),
@@ -135,13 +126,10 @@
             pltpu.VMEM((2, 320, 128), f32),
             pltpu.VMEM((2, 320, 128), bf16),
             pltpu.VMEM((8192, 512), bf16),
-            pltpu.VMEM((8192, 512), bf16),
             pltpu.VMEM((4, 128, 512), f32),
-            pltpu.VMEM((4, 128, 512), bf16),
             pltpu.SemaphoreType.DMA((4,)),
             pltpu.SemaphoreType.DMA((4,)),
             pltpu.SemaphoreType.DMA((11,)),
-            pltpu.SemaphoreType.DMA((9,)),
         ],
         compiler_params=pltpu.CompilerParams(collective_id=1, has_side_effects=True, vmem_limit_bytes=26 << 20),
         name="audio",
@@ -340,7 +328,7 @@
     out[0:32, :] = jnp.zeros((32, 512), bf16)
     out[288:320, :] = jnp.zeros((32, 512), bf16)
     for c in range(4):
-        out[32:288, 128 * c:128 * c + 128] = out32[c].astype(bf16)
+        out[32:288, 128 * c:128 * c + 128] = out32[c, 0:256, :].astype(bf16)
 
 
 def encode(lens, order, utts, taps, weights, bias, gain, shift, pgain, pshift):
@@ -351,7 +339,7 @@
         in_specs=[SM, SM] + [VM] * 8,
         out_specs=VM,
         scratch_shapes=[
-            pltpu.VMEM((1296, 128), f32),
+            pltpu.VMEM((1456, 128), f32),
             pltpu.VMEM((512, 128), bf16),
             pltpu.VMEM((512, 512), f32),
             pltpu.VMEM((512, 512), f32),
@@ -362,7 +350,7 @@
             pltpu.VMEM((4 * 128, 1024), bf16),
             pltpu.VMEM((2 * 128, 1024), bf16),
             pltpu.VMEM((64, 512), f32),
-            pltpu.VMEM((4, 256, 128), f32),
+            pltpu.VMEM((4, 264, 128), f32),
         ],
         compiler_params=pltpu.CompilerParams(vmem_limit_bytes=30 << 20),
         name="encode",

time: 83.2 us -> 82.2 us (0.988)
  the two profiles are of different devices: /device:TPU:71 before, /device:TPU:33 now
where the time goes in v5:
time: 82.2 us; the launch traced here: 82.1 us
  Pallas kernels  81.8 us (100%)
    pallas_call x1, Pallas kernels, encode(): pl.pallas_call(encoder_kernel, out_shape=jax.ShapeDtypeStruct((320, 512),...  29.4 us
    pallas_call x1, Pallas kernels, exchange_frames(): pl.pallas_call(frames_kernel, out_shape=jax.ShapeDtypeStruct((8, 64, 512)...  28.7 us
    pallas_call x1, Pallas kernels, conform(): pl.pallas_call(conformer_kernel, out_shape=jax.ShapeDtypeStruct((4, 64, 1...  14.5 us
    pallas_call x1, Pallas kernels, exchange_audio(): pl.pallas_call(audio_kernel, out_shape=(jax.ShapeDtypeStruct((4, 320, 128...  9.17 us

profile of v5, /device:TPU:33, one launch (start us, length us, event | category | flops | bytes accessed | tf_op | source)
XLA Modules:
  0.0 82.1 jit_solution(10197278566392999319)
XLA Ops:
  0.0 0.0 copy-start.7
  0.0 0.0 copy-start.11
  0.0 0.0 copy-start.10
  0.0 0.0 copy-start.4
  0.0 0.0 copy-start.3
  0.0 0.0 copy-start.9
  0.0 0.0 slice-start
  0.1 9.2 %audio.1 = (bf16[4,320,128]{2,1,0:T(8,128)(2,1)S(1)}, bf16[8192,512]{1,0:T(8,128)(2,1)S(1)}, bf16[4,128,512]{2,1,0:T(8,128)(2,1)S(1)}, f32[7,512]{1,0:T(8,128)S(1)}) custom-call(f32[2,40960]{1,0:T(2,128)} %waves_in.1, f32[10,512]{1,0:T(8,128)} %first_in.1, bf16[6144,512]{1,0:T(8,128)(2,1)} %bitcast.12, bf16[2048,512]{1,0:T(8,128)(2,1)} %bitcast.13, ...), custom_call_target="tpu_custom_call" | custom-call | tf_op jit(solution)/shard_map/audio/pallas_call | solution.py:116
  9.2 0.0 copy-start
  9.2 0.0 copy-start.1
  9.3 0.0 copy-start.2
  9.3 0.0 copy-start.5
  9.3 0.0 copy-start.6
  9.3 0.0 copy-start.8
  9.3 0.0 copy-done.7
  9.3 0.0 copy-done.11
  9.3 0.0 copy-done.10
  9.3 0.0 copy-done.4
  9.3 0.0 copy-done.3
  9.4 0.0 copy-done.9
  9.4 0.0 slice-start.1
  9.4 29.4 %encode.1.frames = bf16[320,512]{1,0:T(8,128)(2,1)S(1)} custom-call(s32[4,4]{1,0:T(4,128)S(1)} %copy-done.7, s32[4,4]{1,0:T(4,128)S(1)} %copy-done.9, bf16[4,320,128]{2,1,0:T(8,128)(2,1)S(1)} %get-tuple-element.9.utts, bf16[4,128,512]{2,1,0:T(8,128)(2,1)S(1)} %get-tuple-element.10.taps, bf16[8192,512]{1,0:T(8,128)(2,1)S(1)} %get-tuple-element.11.w, ...), custom_call_target="tpu_custom_call" | custom-call | tf_op jit(solution)/shard_map/encode/pallas_call | solution.py:336
  38.8 28.7 %frames.1.recv = bf16[8,64,512]{2,1,0:T(8,128)(2,1)S(1)} custom-call(bf16[320,512]{1,0:T(8,128)(2,1)S(1)} %encode.1.frames), custom_call_target="tpu_custom_call" | custom-call | tf_op jit(solution)/shard_map/frames/pallas_call | solution.py:390
  67.5 0.0 slice-done
  67.5 0.0 copy-done
  67.5 0.0 copy-done.1
  67.5 0.0 copy-done.2
  67.5 0.0 copy-done.5
  67.5 0.0 copy-done.6
  67.6 0.0 copy-done.8
  67.6 0.0 slice-done.1
  67.6 14.5 %conform.1 = bf16[4,64,1024]{2,1,0:T(8,128)(2,1)} custom-call(s32[4,4]{1,0:T(4,128)S(1)} %copy-done.7, bf16[8,64,512]{2,1,0:T(8,128)(2,1)S(1)} %frames.1.recv, bf16[512,1024]{1,0:T(8,128)(2,1)S(1)} %copy-done.1, f32[1,1024]{1,0:T(1,128)S(1)} %bitcast.9, f32[2,1024]{1,0:T(2,128)S(1)} %copy-done.5, bf16[2,1024,2048]{2,1,0:T(8,128)(2,1)S(1)} %bitcast.7, ...), custom_call_target="tpu_custom_call" | custom-call | tf_op jit(solution)/shard_map/conform/pallas_call | solution.py:482
  (1 shorter events, 0.0 us)
Async XLA Ops:
  0.0 9.3 %copy-start.7 = (s32[4,4]{1,0:T(4,128)S(1)}, s32[4,4]{1,0:T(4,128)}, u32[]{:S(2)}) copy-start(s32[4,4]{1,0:T(4,128)} %lens.3) | copy-start | bytes 196
  0.0 9.3 %copy-start.11 = (f32[512]{0:T(512)S(1)}, f32[512]{0:T(512)}, u32[]{:S(2)}) copy-start(f32[512]{0:T(512)} %param.28) | copy-start | bytes 6148
  0.0 9.3 %copy-start.10 = (f32[512]{0:T(512)S(1)}, f32[512]{0:T(512)}, u32[]{:S(2)}) copy-start(f32[512]{0:T(512)} %param.27) | copy-start | bytes 6148
  0.0 9.3 %copy-start.4 = (f32[7,512]{1,0:T(8,128)S(1)}, f32[7,512]{1,0:T(8,128)}, u32[]{:S(2)}) copy-start(f32[7,512]{1,0:T(8,128)} %shift.1) | copy-start | bytes 43012
  0.0 9.3 %copy-start.3 = (f32[7,512]{1,0:T(8,128)S(1)}, f32[7,512]{1,0:T(8,128)}, u32[]{:S(2)}) copy-start(f32[7,512]{1,0:T(8,128)} %gain.2) | copy-start | bytes 43012
  0.0 9.3 %copy-start.9 = (s32[4,4]{1,0:T(4,128)S(1)}, s32[4,4]{1,0:T(4,128)}, u32[]{:S(2)}) copy-start(s32[4,4]{1,0:T(4,128)} %order.1) | copy-start | bytes 196
  0.0 67.5 %slice-start = ((s8[8388608]{0:T(1024)(128)(4,1)}), s8[4194304]{0:T(1024)(128)(4,1)S(1)}, s32[]{:S(2)}) async-start(s8[8388608]{0:T(1024)(128)(4,1)} %bitcast.6), calls=%async_computation | async-start | bytes 8388608
  9.2 58.3 %copy-start = (bf16[2,1024,1024]{2,1,0:T(8,128)(2,1)S(1)}, bf16[2,1024,1024]{2,1,0:T(8,128)(2,1)}, u32[]{:S(2)}) copy-start(bf16[2,1024,1024]{2,1,0:T(8,128)(2,1)} %down.1) | copy-start | bytes 12582916
  9.2 58.3 %copy-start.1 = (bf16[512,1024]{1,0:T(8,128)(2,1)S(1)}, bf16[512,1024]{1,0:T(8,128)(2,1)}, u32[]{:S(2)}) copy-start(bf16[512,1024]{1,0:T(8,128)(2,1)} %wp.1) | copy-start | bytes 3145732
  9.3 58.3 %copy-start.2 = (f32[2,31,1024]{2,0,1:T(2,128)S(1)}, f32[2,31,1024]{2,0,1:T(2,128)}, u32[]{:S(2)}) copy-start(f32[2,31,1024]{2,0,1:T(2,128)} %param.33) | copy-start | bytes 761860
  9.3 58.3 %copy-start.5 = (f32[2,1024]{1,0:T(2,128)S(1)}, f32[2,1024]{1,0:T(2,128)}, u32[]{:S(2)}) copy-start(f32[2,1024]{1,0:T(2,128)} %gain.3) | copy-start | bytes 24580
  9.3 58.3 %copy-start.6 = (f32[2,1024]{1,0:T(2,128)S(1)}, f32[2,1024]{1,0:T(2,128)}, u32[]{:S(2)}) copy-start(f32[2,1024]{1,0:T(2,128)} %dbias.1) | copy-start | bytes 24580
  9.3 58.3 %copy-start.8 = (f32[1024]{0:T(1024)S(1)}, f32[1024]{0:T(1024)}, u32[]{:S(2)}) copy-start(f32[1024]{0:T(1024)} %param.30) | copy-start | bytes 12292
  9.4 58.2 %slice-start.1 = ((s8[8388608]{0:T(1024)(128)(4,1)}), s8[4194304]{0:T(1024)(128)(4,1)S(1)}, s32[]{:S(2)}) async-start(s8[8388608]{0:T(1024)(128)(4,1)} %bitcast.6), calls=%async_computation.1 | async-start | bytes 8388608

commit v6 on v5

--- a/solution.py
+++ b/solution.py
@@ -41,13 +41,6 @@
         fetch(b).start()
     small[0].wait()
 
-    def unfold(i, _):
-        for e in range(2):
-            stage[e, pl.ds(i, 1), :] = waves[e:e + 1, pl.ds(pl.multiple_of(128 * i, 128), 128)]
-        return 0
-    lax.fori_loop(0, 320, unfold, 0, unroll=8)
-    held[...] = stage[...].astype(bf16)
-    pl.semaphore_wait(barrier, jnp.where(mine, 3, 4))
     slot = dp % 4
 
     def copy(e, c):
@@ -63,6 +56,13 @@
         return pltpu.make_async_copy(held.at[e], out.at[slot], ssem.at[2 * e + c])
 
     for e in range(2):
+        def unfold(i, _):
+            stage[e, pl.ds(i, 1), :] = waves[e:e + 1, pl.ds(pl.multiple_of(128 * i, 128), 128)]
+            return 0
+        lax.fori_loop(0, 320, unfold, 0, unroll=16)
+        held[e] = stage[e].astype(bf16)
+        if e == 0:
+            pl.semaphore_wait(barrier, jnp.where(mine, 3, 4))
         for c in range(2):
             @pl.when(jnp.logical_not(here(e, c)))
             def _():

time: 82.2 us -> 85.3 us (1.038)
  the two profiles are of different devices: /device:TPU:33 before, /device:TPU:37 now
where the time goes in v6:
time: 85.3 us; the launch traced here: 83.8 us
  Pallas kernels  83.5 us (98%)
    pallas_call x1, Pallas kernels, encode(): pl.pallas_call(encoder_kernel, out_shape=jax.ShapeDtypeStruct((320, 512),...  29.4 us
    pallas_call x1, Pallas kernels, exchange_audio(): pl.pallas_call(audio_kernel, out_shape=(jax.ShapeDtypeStruct((4, 320, 128...  22.5 us
    pallas_call x1, Pallas kernels, exchange_frames(): pl.pallas_call(frames_kernel, out_shape=jax.ShapeDtypeStruct((8, 64, 512)...  17.1 us
    pallas_call x1, Pallas kernels, conform(): pl.pallas_call(conformer_kernel, out_shape=jax.ShapeDtypeStruct((4, 64, 1...  14.5 us

profile of v6, /device:TPU:37, one launch (start us, length us, event | category | flops | bytes accessed | tf_op | source)
XLA Modules:
  0.0 83.8 jit_solution(8132704003746750752)
XLA Ops:
  0.0 0.0 copy-start.7
  0.0 0.0 copy-start.11
  0.0 0.0 copy-start.10
  0.0 0.0 copy-start.4
  0.0 0.0 copy-start.3
  0.0 0.0 copy-start.9
  0.0 0.0 slice-start
  0.1 22.5 %audio.1 = (bf16[4,320,128]{2,1,0:T(8,128)(2,1)S(1)}, bf16[8192,512]{1,0:T(8,128)(2,1)S(1)}, bf16[4,128,512]{2,1,0:T(8,128)(2,1)S(1)}, f32[7,512]{1,0:T(8,128)S(1)}) custom-call(f32[2,40960]{1,0:T(2,128)} %waves_in.1, f32[10,512]{1,0:T(8,128)} %first_in.1, bf16[6144,512]{1,0:T(8,128)(2,1)} %bitcast.12, bf16[2048,512]{1,0:T(8,128)(2,1)} %bitcast.13, ...), custom_call_target="tpu_custom_call" | custom-call | tf_op jit(solution)/shard_map/audio/pallas_call | solution.py:116
  22.6 0.0 copy-start
  22.6 0.0 copy-start.1
  22.6 0.0 copy-start.2
  22.6 0.0 copy-start.5
  22.6 0.0 copy-start.6
  22.6 0.0 copy-start.8
  22.6 0.0 copy-done.7
  22.7 0.0 copy-done.11
  22.7 0.0 copy-done.10
  22.7 0.0 copy-done.4
  22.7 0.0 copy-done.3
  22.7 0.0 copy-done.9
  22.7 0.0 slice-start.1
  22.7 29.4 %encode.1.frames = bf16[320,512]{1,0:T(8,128)(2,1)S(1)} custom-call(s32[4,4]{1,0:T(4,128)S(1)} %copy-done.7, s32[4,4]{1,0:T(4,128)S(1)} %copy-done.9, bf16[4,320,128]{2,1,0:T(8,128)(2,1)S(1)} %get-tuple-element.9.utts, bf16[4,128,512]{2,1,0:T(8,128)(2,1)S(1)} %get-tuple-element.10.taps, bf16[8192,512]{1,0:T(8,128)(2,1)S(1)} %get-tuple-element.11.w, ...), custom_call_target="tpu_custom_call" | custom-call | tf_op jit(solution)/shard_map/encode/pallas_call | solution.py:336
  52.1 17.1 %frames.1.recv = bf16[8,64,512]{2,1,0:T(8,128)(2,1)S(1)} custom-call(bf16[320,512]{1,0:T(8,128)(2,1)S(1)} %encode.1.frames), custom_call_target="tpu_custom_call" | custom-call | tf_op jit(solution)/shard_map/frames/pallas_call | solution.py:390
  69.2 0.0 slice-done
  69.2 0.0 copy-done
  69.2 0.0 copy-done.1
  69.2 0.0 copy-done.2
  69.2 0.0 copy-done.5
  69.3 0.0 copy-done.6
  69.3 0.0 copy-done.8
  69.3 0.0 slice-done.1
  69.3 14.5 %conform.1 = bf16[4,64,1024]{2,1,0:T(8,128)(2,1)} custom-call(s32[4,4]{1,0:T(4,128)S(1)} %copy-done.7, bf16[8,64,512]{2,1,0:T(8,128)(2,1)S(1)} %frames.1.recv, bf16[512,1024]{1,0:T(8,128)(2,1)S(1)} %copy-done.1, f32[1,1024]{1,0:T(1,128)S(1)} %bitcast.9, f32[2,1024]{1,0:T(2,128)S(1)} %copy-done.5, bf16[2,1024,2048]{2,1,0:T(8,128)(2,1)S(1)} %bitcast.7, ...), custom_call_target="tpu_custom_call" | custom-call | tf_op jit(solution)/shard_map/conform/pallas_call | solution.py:482
  (1 shorter events, 0.0 us)
Async XLA Ops:
  0.0 22.6 %copy-start.7 = (s32[4,4]{1,0:T(4,128)S(1)}, s32[4,4]{1,0:T(4,128)}, u32[]{:S(2)}) copy-start(s32[4,4]{1,0:T(4,128)} %lens.3) | copy-start | bytes 196
  0.0 22.7 %copy-start.11 = (f32[512]{0:T(512)S(1)}, f32[512]{0:T(512)}, u32[]{:S(2)}) copy-start(f32[512]{0:T(512)} %param.28) | copy-start | bytes 6148
  0.0 22.7 %copy-start.10 = (f32[512]{0:T(512)S(1)}, f32[512]{0:T(512)}, u32[]{:S(2)}) copy-start(f32[512]{0:T(512)} %param.27) | copy-start | bytes 6148
  0.0 22.7 %copy-start.4 = (f32[7,512]{1,0:T(8,128)S(1)}, f32[7,512]{1,0:T(8,128)}, u32[]{:S(2)}) copy-start(f32[7,512]{1,0:T(8,128)} %shift.1) | copy-start | bytes 43012
  0.0 22.7 %copy-start.3 = (f32[7,512]{1,0:T(8,128)S(1)}, f32[7,512]{1,0:T(8,128)}, u32[]{:S(2)}) copy-start(f32[7,512]{1,0:T(8,128)} %gain.2) | copy-start | bytes 43012
  0.0 22.7 %copy-start.9 = (s32[4,4]{1,0:T(4,128)S(1)}, s32[4,4]{1,0:T(4,128)}, u32[]{:S(2)}) copy-start(s32[4,4]{1,0:T(4,128)} %order.1) | copy-start | bytes 196
  0.0 69.2 %slice-start = ((s8[8388608]{0:T(1024)(128)(4,1)}), s8[4194304]{0:T(1024)(128)(4,1)S(1)}, s32[]{:S(2)}) async-start(s8[8388608]{0:T(1024)(128)(4,1)} %bitcast.6), calls=%async_computation | async-start | bytes 8388608
  22.6 46.6 %copy-start = (bf16[2,1024,1024]{2,1,0:T(8,128)(2,1)S(1)}, bf16[2,1024,1024]{2,1,0:T(8,128)(2,1)}, u32[]{:S(2)}) copy-start(bf16[2,1024,1024]{2,1,0:T(8,128)(2,1)} %down.1) | copy-start | bytes 12582916
  22.6 46.6 %copy-start.1 = (bf16[512,1024]{1,0:T(8,128)(2,1)S(1)}, bf16[512,1024]{1,0:T(8,128)(2,1)}, u32[]{:S(2)}) copy-start(bf16[512,1024]{1,0:T(8,128)(2,1)} %wp.1) | copy-start | bytes 3145732
  22.6 46.6 %copy-start.2 = (f32[2,31,1024]{2,0,1:T(2,128)S(1)}, f32[2,31,1024]{2,0,1:T(2,128)}, u32[]{:S(2)}) copy-start(f32[2,31,1024]{2,0,1:T(2,128)} %param.33) | copy-start | bytes 761860
  22.6 46.6 %copy-start.5 = (f32[2,1024]{1,0:T(2,128)S(1)}, f32[2,1024]{1,0:T(2,128)}, u32[]{:S(2)}) copy-start(f32[2,1024]{1,0:T(2,128)} %gain.3) | copy-start | bytes 24580
  22.6 46.6 %copy-start.6 = (f32[2,1024]{1,0:T(2,128)S(1)}, f32[2,1024]{1,0:T(2,128)}, u32[]{:S(2)}) copy-start(f32[2,1024]{1,0:T(2,128)} %dbias.1) | copy-start | bytes 24580
  22.6 46.6 %copy-start.8 = (f32[1024]{0:T(1024)S(1)}, f32[1024]{0:T(1024)}, u32[]{:S(2)}) copy-start(f32[1024]{0:T(1024)} %param.30) | copy-start | bytes 12292
  22.7 46.6 %slice-start.1 = ((s8[8388608]{0:T(1024)(128)(4,1)}), s8[4194304]{0:T(1024)(128)(4,1)S(1)}, s32[]{:S(2)}) async-start(s8[8388608]{0:T(1024)(128)(4,1)} %bitcast.6), calls=%async_computation.1 | async-start | bytes 8388608
